TPU v7x, 32 devices: a whole 2x2x4 slice. The times are simulated.
32 devices in a mesh: dp: 16 (over z, y, x), mp: 2 (over core).
Axes of the slice: x: 2, y: 2, z: 4, core: 2. Of those that a mesh axis runs over, the one named last changes fastest.
Arguments:
- tokens: bfloat16 [128, 8192], P('mp', 'dp'), may hold values from -6 to 6
- norm_gain: float32 [8192], replicated, may hold values from 0.25 to 1.75
- query_weight: bfloat16 [8192, 2048], P(None, 'dp'), may hold values from -0.0625 to 0.0625
- out_weight: bfloat16 [2048, 8192], P(None, 'dp'), may hold values from -0.125 to 0.125
- gate_scalar: float32 [1], replicated, may hold values from 0.4 to 1.5
- image_keys: bfloat16 [32, 64, 2048], P('mp', None, 'dp'), may hold values from -260 to 260
- image_values: bfloat16 [32, 64, 2048], P('mp', None, 'dp'), may hold values from -6 to 6
- active_image: int32 [32, 4], replicated, may hold values from 0 to 31
- image_slot: int32 [32], replicated, may hold values from 0 to 31, each once
Outputs:
- mixed: bfloat16 [128, 8192], P('mp', 'dp')
Inputs may be any that keep to these rules, and one draw needn't show every extreme that they name: `image_slot`: each slot 0 to 31 once.
All inputs are finite; a program needn't handle non-finite values.
Results may differ from a plain program's by a relative error of at most 0.0047.
Values may be sent and summed in bfloat16 or wider, within the bound.
No kernel may reach another device: no remote copies, remote signals or barrier semaphores. Data moves between devices by JAX's collectives and lax.ppermute only.
A program may use at most 64 MiB of HBM per device.

v0:
```python
import functools

import jax
import jax.numpy as jnp
from jax import lax
from jax.experimental import pallas as pl
from jax.experimental.pallas import tpu as pltpu
from jax.sharding import PartitionSpec as P

epsilon = 1e-05


VMEM = pl.BlockSpec(memory_space=pltpu.VMEM)
SMEM = pl.BlockSpec(memory_space=pltpu.SMEM)
HBM = pl.BlockSpec(memory_space=pltpu.HBM)


def masks(size):
    low = 1 << ((size.bit_length() - 1) // 2)
    far = list(range(low, size, low))
    return far[0], far[1:], list(reversed(range(1, low)))


def exchange(x, axis, size, mask):
    return lax.ppermute(x, axis, [(i, i ^ mask) for i in range(size)])


def gather_wide(x, size):
    first, rest, near = masks(size)
    far = [exchange(x, "dp", size, m) for m in rest]
    head = exchange(x, "dp", size, first)
    side = jnp.stack([exchange(x, "dp", size, m) for m in near])
    far = jnp.stack(far)
    spread = [exchange(far, "dp", size, m) for m in near]
    last = exchange(side, "dp", size, first)
    arrays = [head[None], far, side, *spread, last]
    places = [[first], rest, near, *[[m ^ r for r in rest] for m in near], [first ^ m for m in near]]
    return arrays, places


def gather_small(x, size):
    first, rest, near = masks(size)
    far = [exchange(x, "dp", size, m) for m in rest + [first]]
    column = jnp.stack([x, *far])
    own = [0, *rest, first]
    spread = [exchange(column, "dp", size, m) for m in near]
    return [column, *spread], [own, *[[m ^ o for o in own] for m in near]]


def load_kernel(place_ref, active_ref, slot_ref, *refs):
    count = (len(refs) - 1) // 2
    out_ref, sem = refs[count], refs[-1]
    copies = [
        pltpu.make_async_copy(source, target, sem.at[i])
        for i, (source, target) in enumerate(zip(refs[:count], refs[count + 1 : -1]))
    ]
    for copy in copies:
        copy.start()
    steps = active_ref.shape[0]
    rows, lane = out_ref.shape
    base = place_ref[1] * (rows // steps)
    index = lax.broadcasted_iota(jnp.int32, (8, lane), 0)
    for tile in range(rows // 8):
        block = jnp.zeros((8, lane), jnp.int32)
        for r in range(8):
            row = tile * 8 + r
            block = jnp.where(index == r, slot_ref[active_ref[row % steps, base + row // steps]], block)
        out_ref[tile * 8 : tile * 8 + 8, :] = block
    for copy in copies:
        copy.wait()


def attend_kernel(places, mp, place_ref, *refs):
    tiles = len(places)
    groups, refs = refs[:tiles], refs[tiles:]
    gain_ref, query_ref, wanted_ref = refs[:3]
    keys, values = refs[3 : 3 + mp], refs[3 + mp : 3 + 2 * mp]
    out_ref = refs[-1]
    _, rows, wide = groups[0].shape
    chunks = wide // 128
    order = [(g, i, place) for g, at in zip(groups, places) for i, place in enumerate(at)]
    model = len(order) * wide

    def chunk(g, i, c):
        return g[i, :, c * 128 : c * 128 + 128].astype(jnp.float32)

    total = jnp.zeros((rows, 128), jnp.float32)
    for g, i, _ in order:
        for c in range(chunks):
            total += chunk(g, i, c)
    average = jnp.sum(total, axis=1, keepdims=True) * (1.0 / model)
    total = jnp.zeros((rows, 128), jnp.float32)
    for g, i, _ in order:
        for c in range(chunks):
            centred = chunk(g, i, c) - average
            total += centred * centred
    variance = jnp.sum(total, axis=1, keepdims=True) * (1.0 / model)
    scale = lax.rsqrt(variance + epsilon)

    queries = jnp.zeros((rows, out_ref.shape[1]), jnp.float32)
    for g, i, place in order:
        source = jnp.bitwise_xor(place_ref[0], place)
        normed = [
            ((chunk(g, i, c) - average) * scale * gain_ref[pl.ds(source * chunks + c, 1), :]).astype(jnp.bfloat16)
            for c in range(chunks)
        ]
        weight = query_ref[pl.ds(pl.multiple_of(source * wide, wide), wide), :]
        queries += jnp.dot(jnp.concatenate(normed, axis=1), weight, preferred_element_type=jnp.float32)
    queries = queries.astype(jnp.bfloat16)

    owned, visual, width = keys[0].shape
    columns = owned * visual
    factor = width ** (-0.5)
    wanted = wanted_ref[:, :1]
    scores, matches = [], []
    largest = jnp.full((rows, 1), -1e30, jnp.float32)
    for k in range(mp):
        begin = jnp.bitwise_xor(place_ref[1], k) * owned
        slot = lax.broadcasted_iota(jnp.int32, (1, columns), 1) // visual + begin
        match = wanted == slot
        score = lax.dot_general(
            queries,
            keys[k][...].reshape(columns, width),
            (((1,), (1,)), ((), ())),
            preferred_element_type=jnp.float32,
        )
        score = jnp.where(match, score * factor, -1e30)
        largest = jnp.maximum(largest, jnp.max(score, axis=1, keepdims=True))
        scores.append(score)
        matches.append(match)
    expo = [jnp.where(m, jnp.exp(s - largest), 0.0) for s, m in zip(scores, matches)]
    totals = sum(jnp.sum(e, axis=1, keepdims=True) for e in expo)
    result = jnp.zeros((rows, width), jnp.float32)
    for k in range(mp):
        rounded = (expo[k] / totals).astype(jnp.bfloat16)
        result += jnp.dot(
            rounded, values[k][...].reshape(columns, width), preferred_element_type=jnp.float32
        )
    out_ref[...] = result.astype(jnp.bfloat16)


def project(places, me, groups, weight_ref):
    width = groups[0].shape[2]
    total = None
    for g, at in zip(groups, places):
        for i, place in enumerate(at):
            source = jnp.bitwise_xor(me, place)
            weight = weight_ref[pl.ds(pl.multiple_of(source * width, width), width), :]
            part = jnp.dot(g[i], weight, preferred_element_type=jnp.float32)
            total = part if total is None else total + part
    return total


def own_kernel(places, place_ref, group_ref, weight_ref, out_ref):
    out_ref[...] = project(places, place_ref[0], [group_ref], weight_ref)


def mix_kernel(places, place_ref, gate_ref, *refs):
    groups, (partial_ref, weight_ref, token_ref, out_ref) = refs[:-4], refs[-4:]
    total = partial_ref[...] + project(places, place_ref[0], groups, weight_ref)
    gate = jnp.tanh(jnp.full((1, out_ref.shape[1]), gate_ref[0], jnp.float32))
    out_ref[...] = (token_ref[...].astype(jnp.float32) + gate * total).astype(jnp.bfloat16)


def kernel_call(kernel, limit, shape, in_specs, args, scratch=()):
    return pl.pallas_call(
        kernel,
        out_shape=shape,
        in_specs=in_specs,
        out_specs=jax.tree.map(lambda _: VMEM, shape),
        scratch_shapes=list(scratch),
        compiler_params=pltpu.CompilerParams(vmem_limit_bytes=limit << 20),
    )(*args)


def body(
    dp,
    mp,
    tokens,
    norm_gain,
    query_weight,
    out_weight,
    gate_scalar,
    image_keys,
    image_values,
    active_image,
    image_slot,
):
    rows, _ = tokens.shape
    place = jnp.stack([lax.axis_index("dp"), lax.axis_index("mp")]).astype(jnp.int32)
    arrays, places = gather_wide(tokens, dp)
    keys = [exchange(image_keys, "mp", mp, k) for k in range(1, mp)]
    values = [exchange(image_values, "mp", mp, k) for k in range(1, mp)]

    like = lambda x: jax.ShapeDtypeStruct(x.shape, x.dtype)
    loaded = (tokens, query_weight, image_keys, image_values)
    wanted, own, weight, own_keys, own_values = kernel_call(
        load_kernel,
        1,
        (jax.ShapeDtypeStruct((rows, 128), jnp.int32), *map(like, loaded)),
        [SMEM] * 3 + [HBM] * len(loaded),
        (place, active_image.T, image_slot, *[pltpu.with_memory_space_constraint(x, pltpu.HBM) for x in loaded]),
        [pltpu.SemaphoreType.DMA((len(loaded),))],
    )
    attended = kernel_call(
        functools.partial(attend_kernel, [[0], *places], mp),
        16,
        jax.ShapeDtypeStruct((rows, query_weight.shape[1]), jnp.bfloat16),
        [SMEM] + [VMEM] * (len(arrays) + 4 + 2 * mp),
        (place, own[None], *arrays, norm_gain.reshape(-1, 128), weight, wanted, own_keys, *keys, own_values, *values),
    )
    heads, places = gather_small(attended, dp)
    partial = kernel_call(
        functools.partial(own_kernel, places[:1]),
        4,
        jax.ShapeDtypeStruct(tokens.shape, jnp.float32),
        [SMEM] + [VMEM] * 2,
        (place, heads[0], out_weight),
    )
    return kernel_call(
        functools.partial(mix_kernel, places[1:]),
        4,
        like(tokens),
        [SMEM, SMEM] + [VMEM] * (len(heads) + 2),
        (place, gate_scalar, *heads[1:], partial, out_weight, tokens),
    )


def solution(mesh):
    dp, mp = mesh.shape["dp"], mesh.shape["mp"]
    in_specs = (
        P("mp", "dp"),
        P(),
        P(None, "dp"),
        P(None, "dp"),
        P(),
        P("mp", None, "dp"),
        P("mp", None, "dp"),
        P(),
        P(),
    )

    def step(*args):
        return body(dp, mp, *args)

    return jax.shard_map(step, mesh=mesh, in_specs=in_specs, out_specs=P("mp", "dp"), check_vma=False)
```

profile of v0, /device:TPU:0, one launch (start us, length us, event | category | flops | bytes accessed | tf_op | source)
XLA Modules:
  0.0 42.6 jit_solution(659136299764963370)
XLA Ops:
  0.0 0.0 copy-start.2
  0.0 4.1 %collective-permute-start.1 = (bf16[64,512]{1,0:T(8,128)(2,1)}, bf16[64,512]{1,0:T(8,128)(2,1)S(1)}, u32[]{:S(2)}, u32[]{:S(2)}) collective-permute-start(bf16[64,512]{1,0:T(8,128)(2,1)} %refs_5_.1), channel_id=1, source_target_pairs={{0,16},{2,18},{4,20},{6,22},{8,24},{10,26},{12,28},{14,30},{16,0},... | collective-permute-start | bytes 196616 | tf_op jit(solution)/shard_map/ppermute | solution.py:25
  4.1 1.3 %collective-permute-start.2 = (bf16[64,512]{1,0:T(8,128)(2,1)}, bf16[64,512]{1,0:T(8,128)(2,1)S(1)}, u32[]{:S(2)}, u32[]{:S(2)}) collective-permute-start(bf16[64,512]{1,0:T(8,128)(2,1)} %refs_5_.1), channel_id=1, source_target_pairs={{0,24},{2,26},{4,28},{6,30},{8,16},{10,18},{12,20},{14,22},{16,8},... | collective-permute-start | bytes 196616 | tf_op jit(solution)/shard_map/ppermute | solution.py:25
  5.4 2.4 %collective-permute-start.3 = (bf16[64,512]{1,0:T(8,128)(2,1)}, bf16[64,512]{1,0:T(8,128)(2,1)S(1)}, u32[]{:S(2)}, u32[]{:S(2)}) collective-permute-start(bf16[64,512]{1,0:T(8,128)(2,1)} %refs_5_.1), channel_id=1, source_target_pairs={{0,6},{2,4},{4,2},{6,0},{8,14},{10,12},{12,10},{14,8},{16,22},{18,... | collective-permute-start | bytes 196616 | tf_op jit(solution)/shard_map/ppermute | solution.py:25
  7.9 0.5 %collective-permute-start.4 = (bf16[64,512]{1,0:T(8,128)(2,1)}, bf16[64,512]{1,0:T(8,128)(2,1)S(1)}, u32[]{:S(2)}, u32[]{:S(2)}) collective-permute-start(bf16[64,512]{1,0:T(8,128)(2,1)} %refs_5_.1), channel_id=1, source_target_pairs={{0,4},{2,6},{4,0},{6,2},{8,12},{10,14},{12,8},{14,10},{16,20},{18,... | collective-permute-start | bytes 196616 | tf_op jit(solution)/shard_map/ppermute | solution.py:25
  8.4 0.5 %collective-permute-start.5 = (bf16[64,512]{1,0:T(8,128)(2,1)}, bf16[64,512]{1,0:T(8,128)(2,1)S(1)}, u32[]{:S(2)}, u32[]{:S(2)}) collective-permute-start(bf16[64,512]{1,0:T(8,128)(2,1)} %refs_5_.1), channel_id=1, source_target_pairs={{0,2},{2,0},{4,6},{6,4},{8,10},{10,8},{12,14},{14,12},{16,18},{18,... | collective-permute-start | bytes 196616 | tf_op jit(solution)/shard_map/ppermute | solution.py:25
  8.9 0.0 collective-permute-done.1
  8.9 1.5 %collective-permute-start = (bf16[64,512]{1,0:T(8,128)(2,1)}, bf16[64,512]{1,0:T(8,128)(2,1)S(1)}, u32[]{:S(2)}, u32[]{:S(2)}) collective-permute-start(bf16[64,512]{1,0:T(8,128)(2,1)} %refs_5_.1), channel_id=1, source_target_pairs={{0,8},{2,10},{4,12},{6,14},{8,0},{10,2},{12,4},{14,6},{16,24},{18,... | collective-permute-start | bytes 196616 | tf_op jit(solution)/shard_map/ppermute | solution.py:25
  10.4 0.1 collective-permute-done.2
  10.4 0.0 collective-permute-start.10
  10.5 0.4 %collective-permute-done.3 = bf16[64,512]{1,0:T(8,128)(2,1)S(1)} collective-permute-done((bf16[64,512]{1,0:T(8,128)(2,1)}, bf16[64,512]{1,0:T(8,128)(2,1)S(1)}, u32[]{:S(2)}, u32[]{:S(2)}) %collective-permute-start.3) | collective-permute-done | bytes 65568 | tf_op jit(solution)/shard_map/ppermute | solution.py:25
  10.9 0.2 collective-permute-start.11
  11.0 1.3 %collective-permute-done.4 = bf16[64,512]{1,0:T(8,128)(2,1)S(1)} collective-permute-done((bf16[64,512]{1,0:T(8,128)(2,1)}, bf16[64,512]{1,0:T(8,128)(2,1)S(1)}, u32[]{:S(2)}, u32[]{:S(2)}) %collective-permute-start.4) | collective-permute-done | bytes 65568 | tf_op jit(solution)/shard_map/ppermute | solution.py:25
  12.3 1.2 %collective-permute-start.6 = (bf16[2,64,512]{2,1,0:T(8,128)(2,1)S(1)}, bf16[2,64,512]{2,1,0:T(8,128)(2,1)S(1)}, u32[]{:S(2)}, u32[]{:S(2)}) collective-permute-start(bf16[2,64,512]{2,1,0:T(8,128)(2,1)S(1)} %pad_maximum_fusion.1.refs_2_), channel_id=1, source_target_pairs={{0,6},{2,4},{4,2},{6,0},{8,14},{10,12},{12,10},{14,8},{16,22},{18,... | collective-permute-start | bytes 393224 | tf_op jit(solution)/shard_map/ppermute | solution.py:25
  13.5 0.0 collective-permute-done.5
  13.6 1.1 %collective-permute-start.9 = (bf16[3,64,512]{2,1,0:T(8,128)(2,1)S(1)}, bf16[3,64,512]{2,1,0:T(8,128)(2,1)S(1)}, u32[]{:S(2)}, u32[]{:S(2)}) collective-permute-start(bf16[3,64,512]{2,1,0:T(8,128)(2,1)S(1)} %pad_maximum_fusion.refs_3_), channel_id=1, source_target_pairs={{0,8},{2,10},{4,12},{6,14},{8,0},{10,2},{12,4},{14,6},{16,24},{18,... | collective-permute-start | bytes 589832 | tf_op jit(solution)/shard_map/ppermute | solution.py:25
  14.7 0.0 collective-permute-done
  14.7 0.5 %collective-permute-start.7 = (bf16[2,64,512]{2,1,0:T(8,128)(2,1)S(1)}, bf16[2,64,512]{2,1,0:T(8,128)(2,1)S(1)}, u32[]{:S(2)}, u32[]{:S(2)}) collective-permute-start(bf16[2,64,512]{2,1,0:T(8,128)(2,1)S(1)} %pad_maximum_fusion.1.refs_2_), channel_id=1, source_target_pairs={{0,4},{2,6},{4,0},{6,2},{8,12},{10,14},{12,8},{14,10},{16,20},{18,... | collective-permute-start | bytes 393224 | tf_op jit(solution)/shard_map/ppermute | solution.py:25
  15.2 3.1 %collective-permute-done.6.refs_4_ = bf16[2,64,512]{2,1,0:T(8,128)(2,1)S(1)} collective-permute-done((bf16[2,64,512]{2,1,0:T(8,128)(2,1)S(1)}, bf16[2,64,512]{2,1,0:T(8,128)(2,1)S(1)}, u32[]{:S(2)}, u32[]{:S(2)}) %collective-permute-start.6) | collective-permute-done | bytes 131104 | tf_op jit(solution)/shard_map/ppermute | solution.py:25
  18.3 1.5 %collective-permute-start.8 = (bf16[2,64,512]{2,1,0:T(8,128)(2,1)S(1)}, bf16[2,64,512]{2,1,0:T(8,128)(2,1)S(1)}, u32[]{:S(2)}, u32[]{:S(2)}) collective-permute-start(bf16[2,64,512]{2,1,0:T(8,128)(2,1)S(1)} %pad_maximum_fusion.1.refs_2_), channel_id=1, source_target_pairs={{0,2},{2,0},{4,6},{6,4},{8,10},{10,8},{12,14},{14,12},{16,18},{18,... | collective-permute-start | bytes 393224 | tf_op jit(solution)/shard_map/ppermute | solution.py:25
  19.8 0.1 pad_add_fusion.place_ref
  19.9 0.0 copy-start.3
  19.9 0.7 %copy-done.3 = s32[32,4]{0,1:T(4,128)S(1)} copy-done((s32[32,4]{0,1:T(4,128)S(1)}, s32[32,4]{0,1:T(4,128)}, u32[]{:S(2)}) %copy-start.3) | copy-done | bytes 536
  20.6 0.0 copy-start.4
  20.6 0.7 %copy-done.4 = s32[32]{0:T(128)S(1)} copy-done((s32[32]{0:T(128)S(1)}, s32[32]{0:T(128)}, u32[]{:S(2)}) %copy-start.4) | copy-done | bytes 152
  21.2 2.3 %shard_map.91 = (s32[64,128]{1,0:T(8,128)S(1)}, bf16[64,512]{1,0:T(8,128)(2,1)S(1)}, bf16[8192,128]{1,0:T(8,128)(2,1)S(1)}, bf16[16,64,128]{2,1,0:T(8,128)(2,1)S(1)}, bf16[16,64,128]{2,1,0:T(8,128)(2,1)S(1)}) custom-call(s32[2]{0:T(128)S(1)} %pad_add_fusion.place_ref, s32[4,32]{1,0:T(4,128)S(1)} %bitcast.19, s32[32]{0:T(128)S(1)} %copy-done.4, ...), custom_call_target="tpu_custom_call" | custom-call | tf_op jit(solution)/shard_map/pallas_call | solution.py:166
  23.5 0.0 collective-permute-done.7.refs_5_
  23.5 0.0 collective-permute-done.8.refs_6_
  23.6 0.0 collective-permute-done.9.refs_7_
  23.6 0.0 collective-permute-done.10.refs_12_
  23.6 0.0 collective-permute-done.11.refs_14_
  23.6 0.0 copy-done.2
  23.6 0.0 copy-start
  23.6 2.3 %shard_map.92 = bf16[64,128]{1,0:T(8,128)(2,1)S(1)} custom-call(s32[2]{0:T(128)S(1)} %pad_add_fusion.place_ref, bf16[1,64,512]{2,1,0:T(8,128)(2,1)S(1)} %bitcast.16, bf16[1,64,512]{2,1,0:T(8,128)(2,1)S(1)} %bitcast.15, bf16[2,64,512]{2,1,0:T(8,128)(2,1)S(1)} %pad_maximum_fusion.1.refs_2_, bf16[3,64,512]{2,1,0:T(8,128)(2,1)S(1)} %pad_maximum_fusion.refs_3_, ...), custom_call_target="tpu_custom_call" | custom-call | tf_op jit(solution)/shard_map/pallas_call | solution.py:166
  26.0 0.0 copy-start.1
  26.0 2.5 %collective-permute-start.12 = (bf16[64,128]{1,0:T(8,128)(2,1)S(1)}, bf16[64,128]{1,0:T(8,128)(2,1)S(1)}, u32[]{:S(2)}, u32[]{:S(2)}) collective-permute-start(bf16[64,128]{1,0:T(8,128)(2,1)S(1)} %shard_map.92), channel_id=1, source_target_pairs={{0,16},{2,18},{4,20},{6,22},{8,24},{10,26},{12,28},{14,30},{16,0},... | collective-permute-start | bytes 49160 | tf_op jit(solution)/shard_map/ppermute | solution.py:25
  28.5 0.2 collective-permute-start.13
  28.7 0.8 %collective-permute-start.14 = (bf16[64,128]{1,0:T(8,128)(2,1)S(1)}, bf16[64,128]{1,0:T(8,128)(2,1)S(1)}, u32[]{:S(2)}, u32[]{:S(2)}) collective-permute-start(bf16[64,128]{1,0:T(8,128)(2,1)S(1)} %shard_map.92), channel_id=1, source_target_pairs={{0,8},{2,10},{4,12},{6,14},{8,0},{10,2},{12,4},{14,6},{16,24},{18,... | collective-permute-start | bytes 49160 | tf_op jit(solution)/shard_map/ppermute | solution.py:25
  29.5 1.1 %collective-permute-done.12 = bf16[64,128]{1,0:T(8,128)(2,1)S(1)} collective-permute-done((bf16[64,128]{1,0:T(8,128)(2,1)S(1)}, bf16[64,128]{1,0:T(8,128)(2,1)S(1)}, u32[]{:S(2)}, u32[]{:S(2)}) %collective-permute-start.12) | collective-permute-done | bytes 16416 | tf_op jit(solution)/shard_map/ppermute | solution.py:25
  30.7 3.3 %collective-permute-done.13 = bf16[64,128]{1,0:T(8,128)(2,1)S(1)} collective-permute-done((bf16[64,128]{1,0:T(8,128)(2,1)S(1)}, bf16[64,128]{1,0:T(8,128)(2,1)S(1)}, u32[]{:S(2)}, u32[]{:S(2)}) %collective-permute-start.13) | collective-permute-done | bytes 16416 | tf_op jit(solution)/shard_map/ppermute | solution.py:25
  34.0 0.0 collective-permute-done.14
  34.0 2.2 %collective-permute-start.15 = (bf16[4,64,128]{2,1,0:T(8,128)(2,1)S(1)}, bf16[4,64,128]{2,1,0:T(8,128)(2,1)S(1)}, u32[]{:S(2)}, u32[]{:S(2)}) collective-permute-start(bf16[4,64,128]{2,1,0:T(8,128)(2,1)S(1)} %pad_maximum_fusion.2.group_ref), channel_id=1, source_target_pairs={{0,6},{2,4},{4,2},{6,0},{8,14},{10,12},{12,10},{14,8},{16,22},{18,... | collective-permute-start | bytes 196616 | tf_op jit(solution)/shard_map/ppermute | solution.py:25
  36.2 0.5 %collective-permute-start.16 = (bf16[4,64,128]{2,1,0:T(8,128)(2,1)S(1)}, bf16[4,64,128]{2,1,0:T(8,128)(2,1)S(1)}, u32[]{:S(2)}, u32[]{:S(2)}) collective-permute-start(bf16[4,64,128]{2,1,0:T(8,128)(2,1)S(1)} %pad_maximum_fusion.2.group_ref), channel_id=1, source_target_pairs={{0,4},{2,6},{4,0},{6,2},{8,12},{10,14},{12,8},{14,10},{16,20},{18,... | collective-permute-start | bytes 196616 | tf_op jit(solution)/shard_map/ppermute | solution.py:25
  36.8 0.8 %collective-permute-start.17 = (bf16[4,64,128]{2,1,0:T(8,128)(2,1)S(1)}, bf16[4,64,128]{2,1,0:T(8,128)(2,1)S(1)}, u32[]{:S(2)}, u32[]{:S(2)}) collective-permute-start(bf16[4,64,128]{2,1,0:T(8,128)(2,1)S(1)} %pad_maximum_fusion.2.group_ref), channel_id=1, source_target_pairs={{0,2},{2,0},{4,6},{6,4},{8,10},{10,8},{12,14},{14,12},{16,18},{18,... | collective-permute-start | bytes 196616 | tf_op jit(solution)/shard_map/ppermute | solution.py:25
  38.2 0.0 copy-done
  38.2 0.8 %shard_map.93.refs_3_ = f32[64,512]{1,0:T(8,128)S(1)} custom-call(s32[2]{0:T(128)S(1)} %pad_add_fusion.place_ref, bf16[4,64,128]{2,1,0:T(8,128)(2,1)S(1)} %pad_maximum_fusion.2.group_ref, bf16[2048,512]{1,0:T(8,128)(2,1)S(1)} %copy-done), custom_call_target="tpu_custom_call" | custom-call | tf_op jit(solution)/shard_map/pallas_call | solution.py:166
  39.0 0.3 collective-permute-done.15.refs_0_
  39.3 1.3 %collective-permute-done.16.refs_1_ = bf16[4,64,128]{2,1,0:T(8,128)(2,1)S(1)} collective-permute-done((bf16[4,64,128]{2,1,0:T(8,128)(2,1)S(1)}, bf16[4,64,128]{2,1,0:T(8,128)(2,1)S(1)}, u32[]{:S(2)}, u32[]{:S(2)}) %collective-permute-start.16) | collective-permute-done | bytes 65568 | tf_op jit(solution)/shard_map/ppermute | solution.py:25
  40.5 0.5 %collective-permute-done.17.refs_2_ = bf16[4,64,128]{2,1,0:T(8,128)(2,1)S(1)} collective-permute-done((bf16[4,64,128]{2,1,0:T(8,128)(2,1)S(1)}, bf16[4,64,128]{2,1,0:T(8,128)(2,1)S(1)}, u32[]{:S(2)}, u32[]{:S(2)}) %collective-permute-start.17) | collective-permute-done | bytes 65568 | tf_op jit(solution)/shard_map/ppermute | solution.py:25
  41.0 0.0 copy-done.1
  41.0 1.5 %shard_map.94 = bf16[64,512]{1,0:T(8,128)(2,1)} custom-call(s32[2]{0:T(128)S(1)} %pad_add_fusion.place_ref, f32[1]{0:T(128)S(6)} %copy.10.gate_ref, bf16[4,64,128]{2,1,0:T(8,128)(2,1)S(1)} %collective-permute-done.15.refs_0_, bf16[4,64,128]{2,1,0:T(8,128)(2,1)S(1)} %collective-permute-done.16.refs_1_, ...), custom_call_target="tpu_custom_call" | custom-call | tf_op jit(solution)/shard_map/pallas_call | solution.py:166
  (3 shorter events, 0.0 us)
Async XLA Ops:
  0.0 23.6 %copy-start.2 = (f32[8192]{0:T(1024)S(1)}, f32[8192]{0:T(1024)}, u32[]{:S(2)}) copy-start(f32[8192]{0:T(1024)} %param.10) | copy-start | bytes 98308
  0.0 8.9 %collective-permute-start.1 = (bf16[64,512]{1,0:T(8,128)(2,1)}, bf16[64,512]{1,0:T(8,128)(2,1)S(1)}, u32[]{:S(2)}, u32[]{:S(2)}) collective-permute-start(bf16[64,512]{1,0:T(8,128)(2,1)} %refs_5_.1), channel_id=1, source_target_pairs={{0,16},{2,18},{4,20},{6,22},{8,24},{10,26},{12,28},{14,30},{16,0},... | collective-permute-start | bytes 196616 | tf_op jit(solution)/shard_map/ppermute | solution.py:25
  4.1 6.4 %collective-permute-start.2 = (bf16[64,512]{1,0:T(8,128)(2,1)}, bf16[64,512]{1,0:T(8,128)(2,1)S(1)}, u32[]{:S(2)}, u32[]{:S(2)}) collective-permute-start(bf16[64,512]{1,0:T(8,128)(2,1)} %refs_5_.1), channel_id=1, source_target_pairs={{0,24},{2,26},{4,28},{6,30},{8,16},{10,18},{12,20},{14,22},{16,8},... | collective-permute-start | bytes 196616 | tf_op jit(solution)/shard_map/ppermute | solution.py:25
  5.4 5.5 %collective-permute-start.3 = (bf16[64,512]{1,0:T(8,128)(2,1)}, bf16[64,512]{1,0:T(8,128)(2,1)S(1)}, u32[]{:S(2)}, u32[]{:S(2)}) collective-permute-start(bf16[64,512]{1,0:T(8,128)(2,1)} %refs_5_.1), channel_id=1, source_target_pairs={{0,6},{2,4},{4,2},{6,0},{8,14},{10,12},{12,10},{14,8},{16,22},{18,... | collective-permute-start | bytes 196616 | tf_op jit(solution)/shard_map/ppermute | solution.py:25
  7.9 4.5 %collective-permute-start.4 = (bf16[64,512]{1,0:T(8,128)(2,1)}, bf16[64,512]{1,0:T(8,128)(2,1)S(1)}, u32[]{:S(2)}, u32[]{:S(2)}) collective-permute-start(bf16[64,512]{1,0:T(8,128)(2,1)} %refs_5_.1), channel_id=1, source_target_pairs={{0,4},{2,6},{4,0},{6,2},{8,12},{10,14},{12,8},{14,10},{16,20},{18,... | collective-permute-start | bytes 196616 | tf_op jit(solution)/shard_map/ppermute | solution.py:25
  8.4 5.2 %collective-permute-start.5 = (bf16[64,512]{1,0:T(8,128)(2,1)}, bf16[64,512]{1,0:T(8,128)(2,1)S(1)}, u32[]{:S(2)}, u32[]{:S(2)}) collective-permute-start(bf16[64,512]{1,0:T(8,128)(2,1)} %refs_5_.1), channel_id=1, source_target_pairs={{0,2},{2,0},{4,6},{6,4},{8,10},{10,8},{12,14},{14,12},{16,18},{18,... | collective-permute-start | bytes 196616 | tf_op jit(solution)/shard_map/ppermute | solution.py:25
  8.9 5.8 %collective-permute-start = (bf16[64,512]{1,0:T(8,128)(2,1)}, bf16[64,512]{1,0:T(8,128)(2,1)S(1)}, u32[]{:S(2)}, u32[]{:S(2)}) collective-permute-start(bf16[64,512]{1,0:T(8,128)(2,1)} %refs_5_.1), channel_id=1, source_target_pairs={{0,8},{2,10},{4,12},{6,14},{8,0},{10,2},{12,4},{14,6},{16,24},{18,... | collective-permute-start | bytes 196616 | tf_op jit(solution)/shard_map/ppermute | solution.py:25
  10.4 13.1 %collective-permute-start.10 = (bf16[16,64,128]{2,1,0:T(8,128)(2,1)}, bf16[16,64,128]{2,1,0:T(8,128)(2,1)S(1)}, u32[]{:S(2)}, u32[]{:S(2)}) collective-permute-start(bf16[16,64,128]{2,1,0:T(8,128)(2,1)} %refs_2_.1), channel_id=1, source_target_pairs={{0,1},{1,0},{2,3},{3,2},{4,5},{5,4},{6,7},{7,6},{8,9},{9,8},{10,11... | collective-permute-start | bytes 786440 | tf_op jit(solution)/shard_map/ppermute | solution.py:25
  10.9 12.7 %collective-permute-start.11 = (bf16[16,64,128]{2,1,0:T(8,128)(2,1)}, bf16[16,64,128]{2,1,0:T(8,128)(2,1)S(1)}, u32[]{:S(2)}, u32[]{:S(2)}) collective-permute-start(bf16[16,64,128]{2,1,0:T(8,128)(2,1)} %refs_3_.1), channel_id=1, source_target_pairs={{0,1},{1,0},{2,3},{3,2},{4,5},{5,4},{6,7},{7,6},{8,9},{9,8},{10,11... | collective-permute-start | bytes 786440 | tf_op jit(solution)/shard_map/ppermute | solution.py:25
  12.3 6.0 %collective-permute-start.6 = (bf16[2,64,512]{2,1,0:T(8,128)(2,1)S(1)}, bf16[2,64,512]{2,1,0:T(8,128)(2,1)S(1)}, u32[]{:S(2)}, u32[]{:S(2)}) collective-permute-start(bf16[2,64,512]{2,1,0:T(8,128)(2,1)S(1)} %pad_maximum_fusion.1.refs_2_), channel_id=1, source_target_pairs={{0,6},{2,4},{4,2},{6,0},{8,14},{10,12},{12,10},{14,8},{16,22},{18,... | collective-permute-start | bytes 393224 | tf_op jit(solution)/shard_map/ppermute | solution.py:25
  13.6 10.0 %collective-permute-start.9 = (bf16[3,64,512]{2,1,0:T(8,128)(2,1)S(1)}, bf16[3,64,512]{2,1,0:T(8,128)(2,1)S(1)}, u32[]{:S(2)}, u32[]{:S(2)}) collective-permute-start(bf16[3,64,512]{2,1,0:T(8,128)(2,1)S(1)} %pad_maximum_fusion.refs_3_), channel_id=1, source_target_pairs={{0,8},{2,10},{4,12},{6,14},{8,0},{10,2},{12,4},{14,6},{16,24},{18,... | collective-permute-start | bytes 589832 | tf_op jit(solution)/shard_map/ppermute | solution.py:25
  14.7 8.9 %collective-permute-start.7 = (bf16[2,64,512]{2,1,0:T(8,128)(2,1)S(1)}, bf16[2,64,512]{2,1,0:T(8,128)(2,1)S(1)}, u32[]{:S(2)}, u32[]{:S(2)}) collective-permute-start(bf16[2,64,512]{2,1,0:T(8,128)(2,1)S(1)} %pad_maximum_fusion.1.refs_2_), channel_id=1, source_target_pairs={{0,4},{2,6},{4,0},{6,2},{8,12},{10,14},{12,8},{14,10},{16,20},{18,... | collective-permute-start | bytes 393224 | tf_op jit(solution)/shard_map/ppermute | solution.py:25
  18.3 5.2 %collective-permute-start.8 = (bf16[2,64,512]{2,1,0:T(8,128)(2,1)S(1)}, bf16[2,64,512]{2,1,0:T(8,128)(2,1)S(1)}, u32[]{:S(2)}, u32[]{:S(2)}) collective-permute-start(bf16[2,64,512]{2,1,0:T(8,128)(2,1)S(1)} %pad_maximum_fusion.1.refs_2_), channel_id=1, source_target_pairs={{0,2},{2,0},{4,6},{6,4},{8,10},{10,8},{12,14},{14,12},{16,18},{18,... | collective-permute-start | bytes 393224 | tf_op jit(solution)/shard_map/ppermute | solution.py:25
  19.9 0.7 %copy-start.3 = (s32[32,4]{0,1:T(4,128)S(1)}, s32[32,4]{0,1:T(4,128)}, u32[]{:S(2)}) copy-start(s32[32,4]{0,1:T(4,128)} %param.16) | copy-start | bytes 1540
  20.6 0.7 %copy-start.4 = (s32[32]{0:T(128)S(1)}, s32[32]{0:T(128)}, u32[]{:S(2)}) copy-start(s32[32]{0:T(128)} %slot_ref.1) | copy-start | bytes 388
  23.6 14.6 %copy-start = (bf16[2048,512]{1,0:T(8,128)(2,1)S(1)}, bf16[2048,512]{1,0:T(8,128)(2,1)}, u32[]{:S(2)}) copy-start(bf16[2048,512]{1,0:T(8,128)(2,1)} %refs_4_.1) | copy-start | bytes 6291460
  26.0 15.1 %copy-start.1 = (bf16[64,512]{1,0:T(8,128)(2,1)S(1)}, bf16[64,512]{1,0:T(8,128)(2,1)}, u32[]{:S(2)}) copy-start(bf16[64,512]{1,0:T(8,128)(2,1)} %refs_5_.1) | copy-start | bytes 196612
  26.0 4.7 %collective-permute-start.12 = (bf16[64,128]{1,0:T(8,128)(2,1)S(1)}, bf16[64,128]{1,0:T(8,128)(2,1)S(1)}, u32[]{:S(2)}, u32[]{:S(2)}) collective-permute-start(bf16[64,128]{1,0:T(8,128)(2,1)S(1)} %shard_map.92), channel_id=1, source_target_pairs={{0,16},{2,18},{4,20},{6,22},{8,24},{10,26},{12,28},{14,30},{16,0},... | collective-permute-start | bytes 49160 | tf_op jit(solution)/shard_map/ppermute | solution.py:25
  28.5 5.5 %collective-permute-start.13 = (bf16[64,128]{1,0:T(8,128)(2,1)S(1)}, bf16[64,128]{1,0:T(8,128)(2,1)S(1)}, u32[]{:S(2)}, u32[]{:S(2)}) collective-permute-start(bf16[64,128]{1,0:T(8,128)(2,1)S(1)} %shard_map.92), channel_id=1, source_target_pairs={{0,24},{2,26},{4,28},{6,30},{8,16},{10,18},{12,20},{14,22},{16,8},... | collective-permute-start | bytes 49160 | tf_op jit(solution)/shard_map/ppermute | solution.py:25
  28.7 5.3 %collective-permute-start.14 = (bf16[64,128]{1,0:T(8,128)(2,1)S(1)}, bf16[64,128]{1,0:T(8,128)(2,1)S(1)}, u32[]{:S(2)}, u32[]{:S(2)}) collective-permute-start(bf16[64,128]{1,0:T(8,128)(2,1)S(1)} %shard_map.92), channel_id=1, source_target_pairs={{0,8},{2,10},{4,12},{6,14},{8,0},{10,2},{12,4},{14,6},{16,24},{18,... | collective-permute-start | bytes 49160 | tf_op jit(solution)/shard_map/ppermute | solution.py:25
  34.0 5.2 %collective-permute-start.15 = (bf16[4,64,128]{2,1,0:T(8,128)(2,1)S(1)}, bf16[4,64,128]{2,1,0:T(8,128)(2,1)S(1)}, u32[]{:S(2)}, u32[]{:S(2)}) collective-permute-start(bf16[4,64,128]{2,1,0:T(8,128)(2,1)S(1)} %pad_maximum_fusion.2.group_ref), channel_id=1, source_target_pairs={{0,6},{2,4},{4,2},{6,0},{8,14},{10,12},{12,10},{14,8},{16,22},{18,... | collective-permute-start | bytes 196616 | tf_op jit(solution)/shard_map/ppermute | solution.py:25
  36.2 4.3 %collective-permute-start.16 = (bf16[4,64,128]{2,1,0:T(8,128)(2,1)S(1)}, bf16[4,64,128]{2,1,0:T(8,128)(2,1)S(1)}, u32[]{:S(2)}, u32[]{:S(2)}) collective-permute-start(bf16[4,64,128]{2,1,0:T(8,128)(2,1)S(1)} %pad_maximum_fusion.2.group_ref), channel_id=1, source_target_pairs={{0,4},{2,6},{4,0},{6,2},{8,12},{10,14},{12,8},{14,10},{16,20},{18,... | collective-permute-start | bytes 196616 | tf_op jit(solution)/shard_map/ppermute | solution.py:25
  36.8 4.3 %collective-permute-start.17 = (bf16[4,64,128]{2,1,0:T(8,128)(2,1)S(1)}, bf16[4,64,128]{2,1,0:T(8,128)(2,1)S(1)}, u32[]{:S(2)}, u32[]{:S(2)}) collective-permute-start(bf16[4,64,128]{2,1,0:T(8,128)(2,1)S(1)} %pad_maximum_fusion.2.group_ref), channel_id=1, source_target_pairs={{0,2},{2,0},{4,6},{6,4},{8,10},{10,8},{12,14},{14,12},{16,18},{18,... | collective-permute-start | bytes 196616 | tf_op jit(solution)/shard_map/ppermute | solution.py:25
where the time goes:
time: 42.7 us; the launch traced here: 42.6 us
  starting transfers between devices  21.9 us (51%)
  waiting for transfers between devices  11.4 us (27%)
  Pallas kernels  6.94 us (16%)
  local copies, waits for them, and re-layouts  1.35 us (3%)
  between operations  0.78 us (2%)
    ppermute x18, starting transfers between devices, exchange(): return lax.ppermute(x, axis, [(i, i ^ mask) for i in range(size)])  21.9 us
    ppermute x18, waiting for transfers between devices, exchange(): return lax.ppermute(x, axis, [(i, i ^ mask) for i in range(size)])  11.4 us
    pallas_call x4, Pallas kernels, kernel_call(): pl.pallas_call(kernel, out_shape=shape, in_specs=in_specs, out_specs=jax....  6.94 us
    unnamed x10, local copies, waits for them, and re-layouts  1.35 us
  transfers between devices with their start and end apart: 18, of which 9 were waited for; matrix products, arithmetic and copies ran while one was open for 0% of the time, Pallas kernels for 7%

commit v1 on v0

v1 whole, which is shorter than its diff:
```python
import functools
import math

import jax
import jax.numpy as jnp
from jax import lax
from jax.experimental import pallas as pl
from jax.experimental.pallas import tpu as pltpu
from jax.sharding import PartitionSpec as P

epsilon = 1e-05
LOG2E = math.log2(math.e)
LOADED = 4
EARLY = 3


VMEM = pl.BlockSpec(memory_space=pltpu.VMEM)
SMEM = pl.BlockSpec(memory_space=pltpu.SMEM)
HBM = pl.BlockSpec(memory_space=pltpu.HBM)


def masks(size):
    low = 1 << ((size.bit_length() - 1) // 2)
    far = list(range(low, size, low))
    return far[0], far[1:], list(reversed(range(1, low)))


def exchange(x, axis, size, mask):
    return lax.ppermute(x, axis, [(i, i ^ mask) for i in range(size)])


def gather_wide(x, size):
    first, rest, near = masks(size)
    far = [exchange(x, "dp", size, m) for m in rest]
    head = exchange(x, "dp", size, first)
    side = jnp.stack([exchange(x, "dp", size, m) for m in near])
    far = jnp.stack(far)
    spread = [exchange(far, "dp", size, m) for m in near]
    last = exchange(side, "dp", size, first)
    arrays = [head[None], far, side, *spread, last]
    places = [[first], rest, near, *[[m ^ r for r in rest] for m in near], [first ^ m for m in near]]
    return arrays, places


def gather_small(x, size):
    first, rest, near = masks(size)
    far = {m: exchange(x, "dp", size, m) for m in [*reversed(rest), first]}
    column = jnp.stack([x, *[far[m] for m in [*rest, first]]])
    own = [0, *rest, first]
    spread = [exchange(column, "dp", size, m) for m in near]
    return [column, *spread], [own, *[[m ^ o for o in own] for m in near]]


def load_kernel(active_ref, slot_ref, *refs):
    count = LOADED
    sources, early = refs[:count], refs[count : -(count + 3)]
    wanted_ref, stats_ref, targets, sem = refs[-(count + 3)], refs[-(count + 2)], refs[-(count + 1) : -1], refs[-1]
    copies = [
        pltpu.make_async_copy(source, target, sem.at[i]) for i, (source, target) in enumerate(zip(sources, targets))
    ]
    for copy in copies:
        copy.start()
    steps = active_ref.shape[0]
    rows, lane = wanted_ref.shape
    base = lax.axis_index("mp") * (rows // steps)
    index = lax.broadcasted_iota(jnp.int32, (8, lane), 0)
    ahead = lax.broadcasted_iota(jnp.int32, (8, lane), 1) // targets[-1].shape[1]
    for tile in range(rows // 8):
        block = jnp.zeros((8, lane), jnp.int32)
        for r in range(8):
            row = tile * 8 + r
            block = jnp.where(index == r, slot_ref[active_ref[row % steps, base + row // steps]], block)
        wanted_ref[tile * 8 : tile * 8 + 8, :] = block - ahead
    copies[0].wait()
    tiles = [targets[0], *[g.at[i] for g in early for i in range(g.shape[0])]]
    wide = tiles[0].shape[1]
    zeros = jnp.zeros((rows, lane), jnp.float32)

    def add(c, total):
        for tile in tiles:
            total += tile[:, pl.ds(pl.multiple_of(c * lane, lane), lane)].astype(jnp.float32)
        return total

    average = jnp.sum(lax.fori_loop(0, wide // lane, add, zeros), axis=1, keepdims=True) * (1.0 / (len(tiles) * wide))

    def square(c, total):
        for tile in tiles:
            centred = tile[:, pl.ds(pl.multiple_of(c * lane, lane), lane)].astype(jnp.float32) - average
            total += centred * centred
        return total

    stats_ref[0] = jnp.broadcast_to(average, (rows, lane))
    stats_ref[1] = lax.fori_loop(0, wide // lane, square, zeros)
    for copy in copies[1:]:
        copy.wait()


def attend_kernel(places, early, mp, *refs):
    tiles = len(places)
    groups, refs = refs[:tiles], refs[tiles:]
    gain_ref, query_ref, wanted_ref, stats_ref = refs[:4]
    keys, values = refs[4 : 4 + mp], refs[4 + mp : 4 + 2 * mp]
    out_ref = refs[-1]
    _, rows, wide = groups[0].shape
    lane = 128
    chunks = wide // lane
    order = [(g, i, place) for g, at in zip(groups, places) for i, place in enumerate(at)]
    late = [(g, i) for g in groups[early:] for i in range(g.shape[0])]
    model = len(order) * wide
    me = lax.axis_index("dp")

    shift = stats_ref[0]
    zeros = jnp.zeros((rows, lane), jnp.float32)

    def gather_stats(c, carry):
        total, squares = carry
        for g, i in late:
            moved = g[i, :, pl.ds(pl.multiple_of(c * lane, lane), lane)].astype(jnp.float32) - shift
            total += moved
            squares += moved * moved
        return total, squares

    total, squares = lax.fori_loop(0, chunks, gather_stats, (zeros, stats_ref[1]))
    offset = jnp.sum(total, axis=1, keepdims=True) * (1.0 / model)
    variance = jnp.sum(squares, axis=1, keepdims=True) * (1.0 / model) - offset * offset
    average = shift + offset
    scale = jnp.broadcast_to(lax.rsqrt(variance + epsilon), (rows, lane))

    queries = jnp.zeros((rows, out_ref.shape[1]), jnp.float32)
    for g, i, place in order:
        source = jnp.bitwise_xor(me, place)
        normed = []
        for c in range(chunks):
            centred = g[i, :, c * lane : c * lane + lane].astype(jnp.float32) - average
            normed.append((centred * scale * gain_ref[pl.ds(source * chunks + c, 1), :]).astype(jnp.bfloat16))
        weight = query_ref[pl.ds(pl.multiple_of(source * wide, wide), wide), :]
        queries += jnp.dot(jnp.concatenate(normed, axis=1), weight, preferred_element_type=jnp.float32)
    queries = queries.astype(jnp.bfloat16)

    owned, visual, width = keys[0].shape
    columns = owned * visual
    factor = width ** (-0.5) * LOG2E
    wanted = wanted_ref[...]
    scores = []
    largest = jnp.full((rows, lane), -1e30, jnp.float32)
    for k in range(mp):
        begin = jnp.bitwise_xor(lax.axis_index("mp"), k) * owned
        score = lax.dot_general(
            queries,
            keys[k][...].reshape(columns, width),
            (((1,), (1,)), ((), ())),
            preferred_element_type=jnp.float32,
        )
        for j in range(columns // lane):
            match = wanted == begin + j * (lane // visual)
            part = jnp.where(match, score[:, j * lane : j * lane + lane], -1e30)
            largest = jnp.maximum(largest, part)
            scores.append(part)
    largest = jnp.broadcast_to(jnp.max(largest, axis=1, keepdims=True), (rows, lane))
    expo = [jnp.exp2((part - largest) * factor) for part in scores]
    share = 1.0 / jnp.sum(sum(expo), axis=1, keepdims=True)
    share = jnp.broadcast_to(share, (rows, lane))
    result = jnp.zeros((rows, width), jnp.float32)
    for k in range(mp):
        parts = expo[k * (columns // lane) : (k + 1) * (columns // lane)]
        rounded = jnp.concatenate([(part * share).astype(jnp.bfloat16) for part in parts], axis=1)
        result += jnp.dot(rounded, values[k][...].reshape(columns, width), preferred_element_type=jnp.float32)
    out_ref[...] = result.astype(jnp.bfloat16)


def project(places, groups, weight_ref):
    width = groups[0].shape[2]
    total = None
    for g, at in zip(groups, places):
        for i, place in enumerate(at):
            source = jnp.bitwise_xor(lax.axis_index("dp"), place)
            weight = weight_ref[pl.ds(pl.multiple_of(source * width, width), width), :]
            part = jnp.dot(g[i], weight, preferred_element_type=jnp.float32)
            total = part if total is None else total + part
    return total


def own_kernel(places, gate_ref, group_ref, weight_ref, token_ref, out_ref, tanh_ref):
    gate = jnp.tanh(jnp.full((1, out_ref.shape[1]), gate_ref[0], jnp.float32))
    out_ref[...] = token_ref[...].astype(jnp.float32) + gate * project(places, [group_ref], weight_ref)
    tanh_ref[...] = jnp.broadcast_to(gate, tanh_ref.shape)


def mix_kernel(places, *refs):
    groups, (partial_ref, tanh_ref, weight_ref, out_ref) = refs[:-4], refs[-4:]
    total = project(places, groups, weight_ref)
    out_ref[...] = (partial_ref[...] + tanh_ref[:1, :] * total).astype(jnp.bfloat16)


def kernel_call(kernel, limit, shape, in_specs, args, scratch=()):
    return pl.pallas_call(
        kernel,
        out_shape=shape,
        in_specs=in_specs,
        out_specs=jax.tree.map(lambda _: VMEM, shape),
        scratch_shapes=list(scratch),
        compiler_params=pltpu.CompilerParams(vmem_limit_bytes=limit << 20),
    )(*args)


def body(
    dp,
    mp,
    tokens,
    norm_gain,
    query_weight,
    out_weight,
    gate_scalar,
    image_keys,
    image_values,
    active_image,
    image_slot,
):
    rows = tokens.shape[0]
    arrays, places = gather_wide(tokens, dp)
    keys = [exchange(image_keys, "mp", mp, k) for k in range(1, mp)]
    values = [exchange(image_values, "mp", mp, k) for k in range(1, mp)]

    like = lambda x: jax.ShapeDtypeStruct(x.shape, x.dtype)
    floats = lambda *shape: jax.ShapeDtypeStruct(shape, jnp.float32)
    loaded = (tokens, query_weight, image_keys, image_values)
    wanted, stats, own, weight, own_keys, own_values = kernel_call(
        load_kernel,
        1,
        (jax.ShapeDtypeStruct((rows, 128), jnp.int32), floats(2, rows, 128), *map(like, loaded)),
        [SMEM] * 2 + [HBM] * LOADED + [VMEM] * EARLY,
        (active_image.T, image_slot, *[pltpu.with_memory_space_constraint(x, pltpu.HBM) for x in loaded], *arrays[:EARLY]),
        [pltpu.SemaphoreType.DMA((LOADED,))],
    )
    attended = kernel_call(
        functools.partial(attend_kernel, [[0], *places], EARLY + 1, mp),
        16,
        jax.ShapeDtypeStruct((rows, query_weight.shape[1]), jnp.bfloat16),
        [VMEM] * (len(arrays) + 5 + 2 * mp),
        (own[None], *arrays, norm_gain.reshape(-1, 128), weight, wanted, stats, own_keys, *keys, own_values, *values),
    )
    heads, places = gather_small(attended, dp)
    partial, gate = kernel_call(
        functools.partial(own_kernel, places[:1]),
        4,
        (floats(*tokens.shape), floats(8, tokens.shape[1])),
        [SMEM] + [VMEM] * 3,
        (gate_scalar, heads[0], out_weight, tokens),
    )
    return kernel_call(
        functools.partial(mix_kernel, places[1:]),
        4,
        like(tokens),
        [VMEM] * (len(heads) + 2),
        (*heads[1:], partial, gate, out_weight),
    )


def solution(mesh):
    dp, mp = mesh.shape["dp"], mesh.shape["mp"]
    in_specs = (
        P("mp", "dp"),
        P(),
        P(None, "dp"),
        P(None, "dp"),
        P(),
        P("mp", None, "dp"),
        P("mp", None, "dp"),
        P(),
        P(),
    )

    def step(*args):
        return body(dp, mp, *args)

    return jax.shard_map(step, mesh=mesh, in_specs=in_specs, out_specs=P("mp", "dp"), check_vma=False)
```

time: 42.7 us -> 41.3 us (0.967)
  Pallas kernels: 6.94 us -> 5 us
  waiting for transfers between devices: 11.4 us -> 12 us
    pallas_call x4, Pallas kernels: 6.94 us -> 5 us  [kernel_call(): pl.pallas_call(kernel, out_shape=shape, in_specs=in_specs, out_specs=jax....]
    ppermute x18, waiting for transfers between devices: 11.4 us -> 12 us  [exchange(): return lax.ppermute(x, axis, [(i, i ^ mask) for i in range(size)])]
  transfers between devices with their start and end apart: 18 -> 18, of which waited for: 9 -> 9; matrix products, arithmetic and copies ran while one was open for 0% -> 0% of each run, Pallas kernels for 7% -> 6%
where the time goes in v1:
time: 41.3 us; the launch traced here: 41.2 us
  starting transfers between devices  21.9 us (53%)
  waiting for transfers between devices  12 us (29%)
  Pallas kernels  5 us (12%)
  local copies, waits for them, and re-layouts  1.35 us (3%)
  between operations  0.78 us (2%)
    ppermute x18, starting transfers between devices, exchange(): return lax.ppermute(x, axis, [(i, i ^ mask) for i in range(size)])  21.9 us
    ppermute x18, waiting for transfers between devices, exchange(): return lax.ppermute(x, axis, [(i, i ^ mask) for i in range(size)])  12 us
    pallas_call x4, Pallas kernels, kernel_call(): pl.pallas_call(kernel, out_shape=shape, in_specs=in_specs, out_specs=jax....  5 us
    unnamed x10, local copies, waits for them, and re-layouts  1.35 us
  transfers between devices with their start and end apart: 18, of which 9 were waited for; matrix products, arithmetic and copies ran while one was open for 0% of the time, Pallas kernels for 6%

profile of v1, /device:TPU:0, one launch (start us, length us, event | category | flops | bytes accessed | tf_op | source)
XLA Modules:
  0.0 41.2 jit_solution(8294158943163077919)
XLA Ops:
  0.0 0.0 copy-start.2
  0.0 4.1 %collective-permute-start.1 = (bf16[64,512]{1,0:T(8,128)(2,1)}, bf16[64,512]{1,0:T(8,128)(2,1)S(1)}, u32[]{:S(2)}, u32[]{:S(2)}) collective-permute-start(bf16[64,512]{1,0:T(8,128)(2,1)} %token_ref.1), channel_id=1, source_target_pairs={{0,16},{2,18},{4,20},{6,22},{8,24},{10,26},{12,28},{14,30},{16,0},... | collective-permute-start | bytes 196616 | tf_op jit(solution)/shard_map/ppermute | solution.py:29
  4.1 1.3 %collective-permute-start.2 = (bf16[64,512]{1,0:T(8,128)(2,1)}, bf16[64,512]{1,0:T(8,128)(2,1)S(1)}, u32[]{:S(2)}, u32[]{:S(2)}) collective-permute-start(bf16[64,512]{1,0:T(8,128)(2,1)} %token_ref.1), channel_id=1, source_target_pairs={{0,24},{2,26},{4,28},{6,30},{8,16},{10,18},{12,20},{14,22},{16,8},... | collective-permute-start | bytes 196616 | tf_op jit(solution)/shard_map/ppermute | solution.py:29
  5.4 2.4 %collective-permute-start.3 = (bf16[64,512]{1,0:T(8,128)(2,1)}, bf16[64,512]{1,0:T(8,128)(2,1)S(1)}, u32[]{:S(2)}, u32[]{:S(2)}) collective-permute-start(bf16[64,512]{1,0:T(8,128)(2,1)} %token_ref.1), channel_id=1, source_target_pairs={{0,6},{2,4},{4,2},{6,0},{8,14},{10,12},{12,10},{14,8},{16,22},{18,... | collective-permute-start | bytes 196616 | tf_op jit(solution)/shard_map/ppermute | solution.py:29
  7.9 0.5 %collective-permute-start.4 = (bf16[64,512]{1,0:T(8,128)(2,1)}, bf16[64,512]{1,0:T(8,128)(2,1)S(1)}, u32[]{:S(2)}, u32[]{:S(2)}) collective-permute-start(bf16[64,512]{1,0:T(8,128)(2,1)} %token_ref.1), channel_id=1, source_target_pairs={{0,4},{2,6},{4,0},{6,2},{8,12},{10,14},{12,8},{14,10},{16,20},{18,... | collective-permute-start | bytes 196616 | tf_op jit(solution)/shard_map/ppermute | solution.py:29
  8.4 0.5 %collective-permute-start.5 = (bf16[64,512]{1,0:T(8,128)(2,1)}, bf16[64,512]{1,0:T(8,128)(2,1)S(1)}, u32[]{:S(2)}, u32[]{:S(2)}) collective-permute-start(bf16[64,512]{1,0:T(8,128)(2,1)} %token_ref.1), channel_id=1, source_target_pairs={{0,2},{2,0},{4,6},{6,4},{8,10},{10,8},{12,14},{14,12},{16,18},{18,... | collective-permute-start | bytes 196616 | tf_op jit(solution)/shard_map/ppermute | solution.py:29
  8.9 0.0 collective-permute-done.1
  8.9 1.5 %collective-permute-start = (bf16[64,512]{1,0:T(8,128)(2,1)}, bf16[64,512]{1,0:T(8,128)(2,1)S(1)}, u32[]{:S(2)}, u32[]{:S(2)}) collective-permute-start(bf16[64,512]{1,0:T(8,128)(2,1)} %token_ref.1), channel_id=1, source_target_pairs={{0,8},{2,10},{4,12},{6,14},{8,0},{10,2},{12,4},{14,6},{16,24},{18,... | collective-permute-start | bytes 196616 | tf_op jit(solution)/shard_map/ppermute | solution.py:29
  10.4 0.1 collective-permute-done.2
  10.4 0.0 collective-permute-start.10
  10.5 0.4 %collective-permute-done.3 = bf16[64,512]{1,0:T(8,128)(2,1)S(1)} collective-permute-done((bf16[64,512]{1,0:T(8,128)(2,1)}, bf16[64,512]{1,0:T(8,128)(2,1)S(1)}, u32[]{:S(2)}, u32[]{:S(2)}) %collective-permute-start.3) | collective-permute-done | bytes 65568 | tf_op jit(solution)/shard_map/ppermute | solution.py:29
  10.9 0.2 collective-permute-start.11
  11.0 1.3 %collective-permute-done.4 = bf16[64,512]{1,0:T(8,128)(2,1)S(1)} collective-permute-done((bf16[64,512]{1,0:T(8,128)(2,1)}, bf16[64,512]{1,0:T(8,128)(2,1)S(1)}, u32[]{:S(2)}, u32[]{:S(2)}) %collective-permute-start.4) | collective-permute-done | bytes 65568 | tf_op jit(solution)/shard_map/ppermute | solution.py:29
  12.3 1.2 %collective-permute-start.6 = (bf16[2,64,512]{2,1,0:T(8,128)(2,1)S(1)}, bf16[2,64,512]{2,1,0:T(8,128)(2,1)S(1)}, u32[]{:S(2)}, u32[]{:S(2)}) collective-permute-start(bf16[2,64,512]{2,1,0:T(8,128)(2,1)S(1)} %pad_maximum_fusion.1.refs_5_.refs_2_), channel_id=1, source_target_pairs={{0,6},{2,4},{4,2},{6,0},{8,14},{10,12},{12,10},{14,8},{16,22},{18,... | collective-permute-start | bytes 393224 | tf_op jit(solution)/shard_map/ppermute | solution.py:29
  13.5 0.0 collective-permute-done.5
  13.6 1.1 %collective-permute-start.9 = (bf16[3,64,512]{2,1,0:T(8,128)(2,1)S(1)}, bf16[3,64,512]{2,1,0:T(8,128)(2,1)S(1)}, u32[]{:S(2)}, u32[]{:S(2)}) collective-permute-start(bf16[3,64,512]{2,1,0:T(8,128)(2,1)S(1)} %pad_maximum_fusion.refs_6_.refs_3_), channel_id=1, source_target_pairs={{0,8},{2,10},{4,12},{6,14},{8,0},{10,2},{12,4},{14,6},{16,24},{18,... | collective-permute-start | bytes 589832 | tf_op jit(solution)/shard_map/ppermute | solution.py:29
  14.7 0.0 collective-permute-done
  14.7 0.5 %collective-permute-start.7 = (bf16[2,64,512]{2,1,0:T(8,128)(2,1)S(1)}, bf16[2,64,512]{2,1,0:T(8,128)(2,1)S(1)}, u32[]{:S(2)}, u32[]{:S(2)}) collective-permute-start(bf16[2,64,512]{2,1,0:T(8,128)(2,1)S(1)} %pad_maximum_fusion.1.refs_5_.refs_2_), channel_id=1, source_target_pairs={{0,4},{2,6},{4,0},{6,2},{8,12},{10,14},{12,8},{14,10},{16,20},{18,... | collective-permute-start | bytes 393224 | tf_op jit(solution)/shard_map/ppermute | solution.py:29
  15.2 3.1 %collective-permute-done.6.refs_4_ = bf16[2,64,512]{2,1,0:T(8,128)(2,1)S(1)} collective-permute-done((bf16[2,64,512]{2,1,0:T(8,128)(2,1)S(1)}, bf16[2,64,512]{2,1,0:T(8,128)(2,1)S(1)}, u32[]{:S(2)}, u32[]{:S(2)}) %collective-permute-start.6) | collective-permute-done | bytes 131104 | tf_op jit(solution)/shard_map/ppermute | solution.py:29
  18.3 1.5 %collective-permute-start.8 = (bf16[2,64,512]{2,1,0:T(8,128)(2,1)S(1)}, bf16[2,64,512]{2,1,0:T(8,128)(2,1)S(1)}, u32[]{:S(2)}, u32[]{:S(2)}) collective-permute-start(bf16[2,64,512]{2,1,0:T(8,128)(2,1)S(1)} %pad_maximum_fusion.1.refs_5_.refs_2_), channel_id=1, source_target_pairs={{0,2},{2,0},{4,6},{6,4},{8,10},{10,8},{12,14},{14,12},{16,18},{18,... | collective-permute-start | bytes 393224 | tf_op jit(solution)/shard_map/ppermute | solution.py:29
  19.8 0.0 copy-start.3
  19.8 0.7 %copy-done.3 = s32[32,4]{0,1:T(4,128)S(1)} copy-done((s32[32,4]{0,1:T(4,128)S(1)}, s32[32,4]{0,1:T(4,128)}, u32[]{:S(2)}) %copy-start.3) | copy-done | bytes 536
  20.5 0.0 copy-start.4
  20.5 0.7 %copy-done.4 = s32[32]{0:T(128)S(1)} copy-done((s32[32]{0:T(128)S(1)}, s32[32]{0:T(128)}, u32[]{:S(2)}) %copy-start.4) | copy-done | bytes 152
  21.1 2.3 %shard_map.91 = (s32[64,128]{1,0:T(8,128)S(1)}, f32[2,64,128]{2,1,0:T(8,128)S(1)}, bf16[64,512]{1,0:T(8,128)(2,1)S(1)}, bf16[8192,128]{1,0:T(8,128)(2,1)S(1)}, b...) custom-call(s32[4,32]{1,0:T(4,128)S(1)} %bitcast.18, s32[32]{0:T(128)S(1)} %copy-done.4, ...), custom_call_target="tpu_custom_call" | custom-call | tf_op jit(solution)/shard_map/pallas_call | solution.py:196
  23.5 0.0 collective-permute-done.7.refs_5_
  23.5 0.0 collective-permute-done.8.refs_6_
  23.5 0.0 collective-permute-done.9.refs_7_
  23.5 0.0 collective-permute-done.10.refs_13_
  23.5 0.0 collective-permute-done.11.refs_15_
  23.5 0.0 copy-done.2
  23.5 0.0 copy-start
  23.5 0.0 copy-start.1
  23.5 1.5 %shard_map.92 = bf16[64,128]{1,0:T(8,128)(2,1)S(1)} custom-call(bf16[1,64,512]{2,1,0:T(8,128)(2,1)S(1)} %bitcast.15, bf16[1,64,512]{2,1,0:T(8,128)(2,1)S(1)} %bitcast.14, bf16[2,64,512]{2,1,0:T(8,128)(2,1)S(1)} %pad_maximum_fusion.1.refs_5_.refs_2_, bf16[3,64,512]{2,1,0:T(8,128)(2,1)S(1)} %pad_maximum_fusion.refs_6_.refs_3_, ...), custom_call_target="tpu_custom_call" | custom-call | tf_op jit(solution)/shard_map/pallas_call | solution.py:196
  25.0 2.5 %collective-permute-start.12 = (bf16[64,128]{1,0:T(8,128)(2,1)S(1)}, bf16[64,128]{1,0:T(8,128)(2,1)S(1)}, u32[]{:S(2)}, u32[]{:S(2)}) collective-permute-start(bf16[64,128]{1,0:T(8,128)(2,1)S(1)} %shard_map.92), channel_id=1, source_target_pairs={{0,16},{2,18},{4,20},{6,22},{8,24},{10,26},{12,28},{14,30},{16,0},... | collective-permute-start | bytes 49160 | tf_op jit(solution)/shard_map/ppermute | solution.py:29
  27.5 0.2 collective-permute-start.13
  27.7 0.8 %collective-permute-start.14 = (bf16[64,128]{1,0:T(8,128)(2,1)S(1)}, bf16[64,128]{1,0:T(8,128)(2,1)S(1)}, u32[]{:S(2)}, u32[]{:S(2)}) collective-permute-start(bf16[64,128]{1,0:T(8,128)(2,1)S(1)} %shard_map.92), channel_id=1, source_target_pairs={{0,8},{2,10},{4,12},{6,14},{8,0},{10,2},{12,4},{14,6},{16,24},{18,... | collective-permute-start | bytes 49160 | tf_op jit(solution)/shard_map/ppermute | solution.py:29
  28.6 1.1 %collective-permute-done.12 = bf16[64,128]{1,0:T(8,128)(2,1)S(1)} collective-permute-done((bf16[64,128]{1,0:T(8,128)(2,1)S(1)}, bf16[64,128]{1,0:T(8,128)(2,1)S(1)}, u32[]{:S(2)}, u32[]{:S(2)}) %collective-permute-start.12) | collective-permute-done | bytes 16416 | tf_op jit(solution)/shard_map/ppermute | solution.py:29
  29.7 3.3 %collective-permute-done.13 = bf16[64,128]{1,0:T(8,128)(2,1)S(1)} collective-permute-done((bf16[64,128]{1,0:T(8,128)(2,1)S(1)}, bf16[64,128]{1,0:T(8,128)(2,1)S(1)}, u32[]{:S(2)}, u32[]{:S(2)}) %collective-permute-start.13) | collective-permute-done | bytes 16416 | tf_op jit(solution)/shard_map/ppermute | solution.py:29
  33.1 0.0 collective-permute-done.14
  33.1 2.3 %collective-permute-start.15 = (bf16[4,64,128]{2,1,0:T(8,128)(2,1)S(1)}, bf16[4,64,128]{2,1,0:T(8,128)(2,1)S(1)}, u32[]{:S(2)}, u32[]{:S(2)}) collective-permute-start(bf16[4,64,128]{2,1,0:T(8,128)(2,1)S(1)} %pad_maximum_fusion.2.group_ref), channel_id=1, source_target_pairs={{0,6},{2,4},{4,2},{6,0},{8,14},{10,12},{12,10},{14,8},{16,22},{18,... | collective-permute-start | bytes 196616 | tf_op jit(solution)/shard_map/ppermute | solution.py:29
  35.4 0.5 %collective-permute-start.16 = (bf16[4,64,128]{2,1,0:T(8,128)(2,1)S(1)}, bf16[4,64,128]{2,1,0:T(8,128)(2,1)S(1)}, u32[]{:S(2)}, u32[]{:S(2)}) collective-permute-start(bf16[4,64,128]{2,1,0:T(8,128)(2,1)S(1)} %pad_maximum_fusion.2.group_ref), channel_id=1, source_target_pairs={{0,4},{2,6},{4,0},{6,2},{8,12},{10,14},{12,8},{14,10},{16,20},{18,... | collective-permute-start | bytes 196616 | tf_op jit(solution)/shard_map/ppermute | solution.py:29
  35.9 0.7 %collective-permute-start.17 = (bf16[4,64,128]{2,1,0:T(8,128)(2,1)S(1)}, bf16[4,64,128]{2,1,0:T(8,128)(2,1)S(1)}, u32[]{:S(2)}, u32[]{:S(2)}) collective-permute-start(bf16[4,64,128]{2,1,0:T(8,128)(2,1)S(1)} %pad_maximum_fusion.2.group_ref), channel_id=1, source_target_pairs={{0,2},{2,0},{4,6},{6,4},{8,10},{10,8},{12,14},{14,12},{16,18},{18,... | collective-permute-start | bytes 196616 | tf_op jit(solution)/shard_map/ppermute | solution.py:29
  37.3 0.0 copy-done
  37.3 0.0 copy-done.1
  37.3 0.2 shard_map.93
  37.5 0.8 %collective-permute-done.15.refs_0_ = bf16[4,64,128]{2,1,0:T(8,128)(2,1)S(1)} collective-permute-done((bf16[4,64,128]{2,1,0:T(8,128)(2,1)S(1)}, bf16[4,64,128]{2,1,0:T(8,128)(2,1)S(1)}, u32[]{:S(2)}, u32[]{:S(2)}) %collective-permute-start.15) | collective-permute-done | bytes 65568 | tf_op jit(solution)/shard_map/ppermute | solution.py:29
  38.3 1.3 %collective-permute-done.16.refs_1_ = bf16[4,64,128]{2,1,0:T(8,128)(2,1)S(1)} collective-permute-done((bf16[4,64,128]{2,1,0:T(8,128)(2,1)S(1)}, bf16[4,64,128]{2,1,0:T(8,128)(2,1)S(1)}, u32[]{:S(2)}, u32[]{:S(2)}) %collective-permute-start.16) | collective-permute-done | bytes 65568 | tf_op jit(solution)/shard_map/ppermute | solution.py:29
  39.6 0.5 %collective-permute-done.17.refs_2_ = bf16[4,64,128]{2,1,0:T(8,128)(2,1)S(1)} collective-permute-done((bf16[4,64,128]{2,1,0:T(8,128)(2,1)S(1)}, bf16[4,64,128]{2,1,0:T(8,128)(2,1)S(1)}, u32[]{:S(2)}, u32[]{:S(2)}) %collective-permute-start.17) | collective-permute-done | bytes 65568 | tf_op jit(solution)/shard_map/ppermute | solution.py:29
  40.2 1.0 %shard_map.94 = bf16[64,512]{1,0:T(8,128)(2,1)} custom-call(bf16[4,64,128]{2,1,0:T(8,128)(2,1)S(1)} %collective-permute-done.15.refs_0_, bf16[4,64,128]{2,1,0:T(8,128)(2,1)S(1)} %collective-permute-done.16.refs_1_, bf16[4,64,128]{2,1,0:T(8,128)(2,1)S(1)} %collective-permute-done.17.refs_2_, f32[64,512]{1,0:T(8,128)S(1)} %get-tuple-element.19.refs_3_, ...), custom_call_target="tpu_custom_call" | custom-call | tf_op jit(solution)/shard_map/pallas_call | solution.py:196
  (3 shorter events, 0.0 us)
Async XLA Ops:
  0.0 23.5 %copy-start.2 = (f32[8192]{0:T(1024)S(1)}, f32[8192]{0:T(1024)}, u32[]{:S(2)}) copy-start(f32[8192]{0:T(1024)} %param.10) | copy-start | bytes 98308
  0.0 8.9 %collective-permute-start.1 = (bf16[64,512]{1,0:T(8,128)(2,1)}, bf16[64,512]{1,0:T(8,128)(2,1)S(1)}, u32[]{:S(2)}, u32[]{:S(2)}) collective-permute-start(bf16[64,512]{1,0:T(8,128)(2,1)} %token_ref.1), channel_id=1, source_target_pairs={{0,16},{2,18},{4,20},{6,22},{8,24},{10,26},{12,28},{14,30},{16,0},... | collective-permute-start | bytes 196616 | tf_op jit(solution)/shard_map/ppermute | solution.py:29
  4.1 6.4 %collective-permute-start.2 = (bf16[64,512]{1,0:T(8,128)(2,1)}, bf16[64,512]{1,0:T(8,128)(2,1)S(1)}, u32[]{:S(2)}, u32[]{:S(2)}) collective-permute-start(bf16[64,512]{1,0:T(8,128)(2,1)} %token_ref.1), channel_id=1, source_target_pairs={{0,24},{2,26},{4,28},{6,30},{8,16},{10,18},{12,20},{14,22},{16,8},... | collective-permute-start | bytes 196616 | tf_op jit(solution)/shard_map/ppermute | solution.py:29
  5.4 5.5 %collective-permute-start.3 = (bf16[64,512]{1,0:T(8,128)(2,1)}, bf16[64,512]{1,0:T(8,128)(2,1)S(1)}, u32[]{:S(2)}, u32[]{:S(2)}) collective-permute-start(bf16[64,512]{1,0:T(8,128)(2,1)} %token_ref.1), channel_id=1, source_target_pairs={{0,6},{2,4},{4,2},{6,0},{8,14},{10,12},{12,10},{14,8},{16,22},{18,... | collective-permute-start | bytes 196616 | tf_op jit(solution)/shard_map/ppermute | solution.py:29
  7.9 4.5 %collective-permute-start.4 = (bf16[64,512]{1,0:T(8,128)(2,1)}, bf16[64,512]{1,0:T(8,128)(2,1)S(1)}, u32[]{:S(2)}, u32[]{:S(2)}) collective-permute-start(bf16[64,512]{1,0:T(8,128)(2,1)} %token_ref.1), channel_id=1, source_target_pairs={{0,4},{2,6},{4,0},{6,2},{8,12},{10,14},{12,8},{14,10},{16,20},{18,... | collective-permute-start | bytes 196616 | tf_op jit(solution)/shard_map/ppermute | solution.py:29
  8.4 5.2 %collective-permute-start.5 = (bf16[64,512]{1,0:T(8,128)(2,1)}, bf16[64,512]{1,0:T(8,128)(2,1)S(1)}, u32[]{:S(2)}, u32[]{:S(2)}) collective-permute-start(bf16[64,512]{1,0:T(8,128)(2,1)} %token_ref.1), channel_id=1, source_target_pairs={{0,2},{2,0},{4,6},{6,4},{8,10},{10,8},{12,14},{14,12},{16,18},{18,... | collective-permute-start | bytes 196616 | tf_op jit(solution)/shard_map/ppermute | solution.py:29
  8.9 5.8 %collective-permute-start = (bf16[64,512]{1,0:T(8,128)(2,1)}, bf16[64,512]{1,0:T(8,128)(2,1)S(1)}, u32[]{:S(2)}, u32[]{:S(2)}) collective-permute-start(bf16[64,512]{1,0:T(8,128)(2,1)} %token_ref.1), channel_id=1, source_target_pairs={{0,8},{2,10},{4,12},{6,14},{8,0},{10,2},{12,4},{14,6},{16,24},{18,... | collective-permute-start | bytes 196616 | tf_op jit(solution)/shard_map/ppermute | solution.py:29
  10.4 13.0 %collective-permute-start.10 = (bf16[16,64,128]{2,1,0:T(8,128)(2,1)}, bf16[16,64,128]{2,1,0:T(8,128)(2,1)S(1)}, u32[]{:S(2)}, u32[]{:S(2)}) collective-permute-start(bf16[16,64,128]{2,1,0:T(8,128)(2,1)} %refs_2_.1), channel_id=1, source_target_pairs={{0,1},{1,0},{2,3},{3,2},{4,5},{5,4},{6,7},{7,6},{8,9},{9,8},{10,11... | collective-permute-start | bytes 786440 | tf_op jit(solution)/shard_map/ppermute | solution.py:29
  10.9 12.6 %collective-permute-start.11 = (bf16[16,64,128]{2,1,0:T(8,128)(2,1)}, bf16[16,64,128]{2,1,0:T(8,128)(2,1)S(1)}, u32[]{:S(2)}, u32[]{:S(2)}) collective-permute-start(bf16[16,64,128]{2,1,0:T(8,128)(2,1)} %refs_3_.1), channel_id=1, source_target_pairs={{0,1},{1,0},{2,3},{3,2},{4,5},{5,4},{6,7},{7,6},{8,9},{9,8},{10,11... | collective-permute-start | bytes 786440 | tf_op jit(solution)/shard_map/ppermute | solution.py:29
  12.3 6.0 %collective-permute-start.6 = (bf16[2,64,512]{2,1,0:T(8,128)(2,1)S(1)}, bf16[2,64,512]{2,1,0:T(8,128)(2,1)S(1)}, u32[]{:S(2)}, u32[]{:S(2)}) collective-permute-start(bf16[2,64,512]{2,1,0:T(8,128)(2,1)S(1)} %pad_maximum_fusion.1.refs_5_.refs_2_), channel_id=1, source_target_pairs={{0,6},{2,4},{4,2},{6,0},{8,14},{10,12},{12,10},{14,8},{16,22},{18,... | collective-permute-start | bytes 393224 | tf_op jit(solution)/shard_map/ppermute | solution.py:29
  13.6 9.9 %collective-permute-start.9 = (bf16[3,64,512]{2,1,0:T(8,128)(2,1)S(1)}, bf16[3,64,512]{2,1,0:T(8,128)(2,1)S(1)}, u32[]{:S(2)}, u32[]{:S(2)}) collective-permute-start(bf16[3,64,512]{2,1,0:T(8,128)(2,1)S(1)} %pad_maximum_fusion.refs_6_.refs_3_), channel_id=1, source_target_pairs={{0,8},{2,10},{4,12},{6,14},{8,0},{10,2},{12,4},{14,6},{16,24},{18,... | collective-permute-start | bytes 589832 | tf_op jit(solution)/shard_map/ppermute | solution.py:29
  14.7 8.8 %collective-permute-start.7 = (bf16[2,64,512]{2,1,0:T(8,128)(2,1)S(1)}, bf16[2,64,512]{2,1,0:T(8,128)(2,1)S(1)}, u32[]{:S(2)}, u32[]{:S(2)}) collective-permute-start(bf16[2,64,512]{2,1,0:T(8,128)(2,1)S(1)} %pad_maximum_fusion.1.refs_5_.refs_2_), channel_id=1, source_target_pairs={{0,4},{2,6},{4,0},{6,2},{8,12},{10,14},{12,8},{14,10},{16,20},{18,... | collective-permute-start | bytes 393224 | tf_op jit(solution)/shard_map/ppermute | solution.py:29
  18.3 5.2 %collective-permute-start.8 = (bf16[2,64,512]{2,1,0:T(8,128)(2,1)S(1)}, bf16[2,64,512]{2,1,0:T(8,128)(2,1)S(1)}, u32[]{:S(2)}, u32[]{:S(2)}) collective-permute-start(bf16[2,64,512]{2,1,0:T(8,128)(2,1)S(1)} %pad_maximum_fusion.1.refs_5_.refs_2_), channel_id=1, source_target_pairs={{0,2},{2,0},{4,6},{6,4},{8,10},{10,8},{12,14},{14,12},{16,18},{18,... | collective-permute-start | bytes 393224 | tf_op jit(solution)/shard_map/ppermute | solution.py:29
  19.8 0.7 %copy-start.3 = (s32[32,4]{0,1:T(4,128)S(1)}, s32[32,4]{0,1:T(4,128)}, u32[]{:S(2)}) copy-start(s32[32,4]{0,1:T(4,128)} %param.16) | copy-start | bytes 1540
  20.5 0.7 %copy-start.4 = (s32[32]{0:T(128)S(1)}, s32[32]{0:T(128)}, u32[]{:S(2)}) copy-start(s32[32]{0:T(128)} %slot_ref.1) | copy-start | bytes 388
  23.5 13.8 %copy-start = (bf16[2048,512]{1,0:T(8,128)(2,1)S(1)}, bf16[2048,512]{1,0:T(8,128)(2,1)}, u32[]{:S(2)}) copy-start(bf16[2048,512]{1,0:T(8,128)(2,1)} %refs_5_.1) | copy-start | bytes 6291460
  23.5 13.8 %copy-start.1 = (bf16[64,512]{1,0:T(8,128)(2,1)S(1)}, bf16[64,512]{1,0:T(8,128)(2,1)}, u32[]{:S(2)}) copy-start(bf16[64,512]{1,0:T(8,128)(2,1)} %token_ref.1) | copy-start | bytes 196612
  25.0 4.7 %collective-permute-start.12 = (bf16[64,128]{1,0:T(8,128)(2,1)S(1)}, bf16[64,128]{1,0:T(8,128)(2,1)S(1)}, u32[]{:S(2)}, u32[]{:S(2)}) collective-permute-start(bf16[64,128]{1,0:T(8,128)(2,1)S(1)} %shard_map.92), channel_id=1, source_target_pairs={{0,16},{2,18},{4,20},{6,22},{8,24},{10,26},{12,28},{14,30},{16,0},... | collective-permute-start | bytes 49160 | tf_op jit(solution)/shard_map/ppermute | solution.py:29
  27.5 5.5 %collective-permute-start.13 = (bf16[64,128]{1,0:T(8,128)(2,1)S(1)}, bf16[64,128]{1,0:T(8,128)(2,1)S(1)}, u32[]{:S(2)}, u32[]{:S(2)}) collective-permute-start(bf16[64,128]{1,0:T(8,128)(2,1)S(1)} %shard_map.92), channel_id=1, source_target_pairs={{0,24},{2,26},{4,28},{6,30},{8,16},{10,18},{12,20},{14,22},{16,8},... | collective-permute-start | bytes 49160 | tf_op jit(solution)/shard_map/ppermute | solution.py:29
  27.7 5.3 %collective-permute-start.14 = (bf16[64,128]{1,0:T(8,128)(2,1)S(1)}, bf16[64,128]{1,0:T(8,128)(2,1)S(1)}, u32[]{:S(2)}, u32[]{:S(2)}) collective-permute-start(bf16[64,128]{1,0:T(8,128)(2,1)S(1)} %shard_map.92), channel_id=1, source_target_pairs={{0,8},{2,10},{4,12},{6,14},{8,0},{10,2},{12,4},{14,6},{16,24},{18,... | collective-permute-start | bytes 49160 | tf_op jit(solution)/shard_map/ppermute | solution.py:29
  33.1 5.2 %collective-permute-start.15 = (bf16[4,64,128]{2,1,0:T(8,128)(2,1)S(1)}, bf16[4,64,128]{2,1,0:T(8,128)(2,1)S(1)}, u32[]{:S(2)}, u32[]{:S(2)}) collective-permute-start(bf16[4,64,128]{2,1,0:T(8,128)(2,1)S(1)} %pad_maximum_fusion.2.group_ref), channel_id=1, source_target_pairs={{0,6},{2,4},{4,2},{6,0},{8,14},{10,12},{12,10},{14,8},{16,22},{18,... | collective-permute-start | bytes 196616 | tf_op jit(solution)/shard_map/ppermute | solution.py:29
  35.4 4.3 %collective-permute-start.16 = (bf16[4,64,128]{2,1,0:T(8,128)(2,1)S(1)}, bf16[4,64,128]{2,1,0:T(8,128)(2,1)S(1)}, u32[]{:S(2)}, u32[]{:S(2)}) collective-permute-start(bf16[4,64,128]{2,1,0:T(8,128)(2,1)S(1)} %pad_maximum_fusion.2.group_ref), channel_id=1, source_target_pairs={{0,4},{2,6},{4,0},{6,2},{8,12},{10,14},{12,8},{14,10},{16,20},{18,... | collective-permute-start | bytes 196616 | tf_op jit(solution)/shard_map/ppermute | solution.py:29
  35.9 4.3 %collective-permute-start.17 = (bf16[4,64,128]{2,1,0:T(8,128)(2,1)S(1)}, bf16[4,64,128]{2,1,0:T(8,128)(2,1)S(1)}, u32[]{:S(2)}, u32[]{:S(2)}) collective-permute-start(bf16[4,64,128]{2,1,0:T(8,128)(2,1)S(1)} %pad_maximum_fusion.2.group_ref), channel_id=1, source_target_pairs={{0,2},{2,0},{4,6},{6,4},{8,10},{10,8},{12,14},{14,12},{16,18},{18,... | collective-permute-start | bytes 196616 | tf_op jit(solution)/shard_map/ppermute | solution.py:29

commit v2 on v1

v2 whole, which is shorter than its diff:
```python
import functools
import math

import jax
import jax.numpy as jnp
from jax import lax
from jax.experimental import pallas as pl
from jax.experimental.pallas import tpu as pltpu
from jax.sharding import PartitionSpec as P

epsilon = 1e-05
LOG2E = math.log2(math.e)
LOADED = 7
EARLY = 3


VMEM = pl.BlockSpec(memory_space=pltpu.VMEM)
SMEM = pl.BlockSpec(memory_space=pltpu.SMEM)
HBM = pl.BlockSpec(memory_space=pltpu.HBM)


def masks(size):
    low = 1 << ((size.bit_length() - 1) // 2)
    far = list(range(low, size, low))
    return far[0], far[1:], list(reversed(range(1, low)))


def exchange(x, axis, size, mask):
    return lax.ppermute(x, axis, [(i, i ^ mask) for i in range(size)])


def gather_wide(x, size):
    first, rest, near = masks(size)
    far = [exchange(x, "dp", size, m) for m in rest]
    head = exchange(x, "dp", size, first)
    side = jnp.stack([exchange(x, "dp", size, m) for m in near])
    far = jnp.stack(far)
    spread = [exchange(far, "dp", size, m) for m in near]
    last = exchange(side, "dp", size, first)
    arrays = [head[None], far, side, *spread, last]
    places = [[first], rest, near, *[[m ^ r for r in rest] for m in near], [first ^ m for m in near]]
    return arrays, places


def gather_small(x, size):
    first, rest, near = masks(size)
    far = {m: exchange(x, "dp", size, m) for m in [*reversed(rest), first]}
    column = jnp.stack([x, *[far[m] for m in [*rest, first]]])
    own = [0, *rest, first]
    spread = [exchange(column, "dp", size, m) for m in near]
    return [column, *spread], [own, *[[m ^ o for o in own] for m in near]]


def rows_of(weight_ref, source, count):
    return weight_ref[pl.ds(pl.multiple_of(source * count, count), count), :]


def load_kernel(*refs):
    early, sources = refs[:EARLY], refs[EARLY : EARLY + LOADED]
    wanted_ref, stats_ref, *targets = refs[EARLY + LOADED : EARLY + 2 * LOADED]
    active_ref, slot_ref, sem = refs[-3:]
    targets += [active_ref, slot_ref]
    copies = [
        pltpu.make_async_copy(source, target, sem.at[i]) for i, (source, target) in enumerate(zip(sources, targets))
    ]
    for copy in copies:
        copy.start()
    own_ref, visual = targets[0], targets[2].shape[1]
    rows, lane = wanted_ref.shape
    wide = own_ref.shape[1]

    copies[0].wait()
    tiles = [own_ref, *[g.at[i] for g in early for i in range(g.shape[0])]]
    zeros = jnp.zeros((rows, lane), jnp.float32)

    def add(c, total):
        for tile in tiles:
            total += tile[:, pl.ds(pl.multiple_of(c * lane, lane), lane)].astype(jnp.float32)
        return total

    average = jnp.sum(lax.fori_loop(0, wide // lane, add, zeros), axis=1, keepdims=True) * (1.0 / (len(tiles) * wide))
    shift = jnp.broadcast_to(average, (rows, lane))
    stats_ref[0] = shift

    for copy in copies[-2:]:
        copy.wait()
    steps = active_ref.shape[0]
    base = lax.axis_index("mp") * (rows // steps)
    index = lax.broadcasted_iota(jnp.int32, (8, lane), 0)
    ahead = lax.broadcasted_iota(jnp.int32, (8, lane), 1) // visual
    for group in range(rows // 8):
        block = jnp.zeros((8, lane), jnp.int32)
        for r in range(8):
            row = group * 8 + r
            block = jnp.where(index == r, slot_ref[active_ref[row % steps, base + row // steps]], block)
        wanted_ref[group * 8 : group * 8 + 8, :] = block - ahead

    squares = zeros
    for tile in tiles:
        for c in range(wide // lane):
            moved = tile[:, c * lane : c * lane + lane].astype(jnp.float32) - shift
            squares += moved * moved
    stats_ref[1] = squares
    for copy in copies[1:-2]:
        copy.wait()


def attend_kernel(places, early, mp, *refs):
    tiles = len(places)
    groups, refs = refs[:tiles], refs[tiles:]
    gain_ref, weight_ref, wanted_ref, stats_ref = refs[:4]
    keys, values = refs[4 : 4 + mp], refs[4 + mp : 4 + 2 * mp]
    out_ref = refs[-1]
    _, rows, wide = groups[0].shape
    lane = wanted_ref.shape[1]
    chunks = wide // lane
    model = weight_ref.shape[0]
    late = [g.at[i] for g in groups[early:] for i in range(g.shape[0])]

    shift = stats_ref[0]

    def add(c, carry):
        total, squares = carry
        for tile in late:
            moved = tile[:, pl.ds(pl.multiple_of(c * lane, lane), lane)].astype(jnp.float32) - shift
            total += moved
            squares += moved * moved
        return total, squares

    total, squares = lax.fori_loop(0, chunks, add, (jnp.zeros((rows, lane), jnp.float32), stats_ref[1]))
    offset = jnp.sum(total, axis=1, keepdims=True) * (1.0 / model)
    variance = jnp.sum(squares, axis=1, keepdims=True) * (1.0 / model) - offset * offset
    average = shift + offset
    scale = jnp.broadcast_to(lax.rsqrt(variance + epsilon), (rows, lane))

    queries = jnp.zeros((rows, out_ref.shape[1]), jnp.float32)
    for g, at in zip(groups, places):
        for i, place in enumerate(at):
            source = jnp.bitwise_xor(lax.axis_index("dp"), place)
            normed = []
            for c in range(chunks):
                centred = g[i, :, c * lane : c * lane + lane].astype(jnp.float32) - average
                normed.append((centred * scale * gain_ref[pl.ds(source * chunks + c, 1), :]).astype(jnp.bfloat16))
            weight = rows_of(weight_ref, source, wide)
            queries += jnp.dot(jnp.concatenate(normed, axis=1), weight, preferred_element_type=jnp.float32)
    queries = queries.astype(jnp.bfloat16)

    owned, visual, width = keys[0].shape
    columns = owned * visual
    factor = width ** (-0.5) * LOG2E
    wanted = wanted_ref[...]
    peaks, sums, expos = [], [], []
    for k in range(mp):
        begin = jnp.bitwise_xor(lax.axis_index("mp"), k) * owned
        score = lax.dot_general(
            queries,
            keys[k][...].reshape(columns, width),
            (((1,), (1,)), ((), ())),
            preferred_element_type=jnp.float32,
        )
        parts = []
        for j in range(columns // lane):
            match = wanted == begin + j * (lane // visual)
            parts.append(jnp.where(match, score[:, j * lane : j * lane + lane], -1e30))
        peak = jnp.max(functools.reduce(jnp.maximum, parts), axis=1, keepdims=True)
        spread = jnp.broadcast_to(peak, (rows, lane))
        expo = [jnp.exp2((part - spread) * factor) for part in parts]
        peaks.append(peak)
        sums.append(jnp.sum(functools.reduce(jnp.add, expo), axis=1, keepdims=True))
        expos.append(expo)
    peak = functools.reduce(jnp.maximum, peaks)
    weights = [jnp.exp2((p - peak) * factor) for p in peaks]
    share = 1.0 / functools.reduce(jnp.add, [w * t for w, t in zip(weights, sums)])
    result = jnp.zeros((rows, width), jnp.float32)
    for k in range(mp):
        times = jnp.broadcast_to(weights[k] * share, (rows, lane))
        rounded = jnp.concatenate([(part * times).astype(jnp.bfloat16) for part in expos[k]], axis=1)
        result += jnp.dot(rounded, values[k][...].reshape(columns, width), preferred_element_type=jnp.float32)
    out_ref[...] = result.astype(jnp.bfloat16)


def project(places, one, two, weight_ref):
    width = one.shape[2]
    me = lax.axis_index("dp")
    total = None
    for i, place in enumerate(places):
        even = jnp.bitwise_and(jnp.bitwise_xor(me, place), 1) == 0
        pair = jnp.concatenate([jnp.where(even, one[i], two[i]), jnp.where(even, two[i], one[i])], axis=1)
        weight = rows_of(weight_ref, jnp.right_shift(jnp.bitwise_xor(me, place), 1), 2 * width)
        part = jnp.dot(pair, weight, preferred_element_type=jnp.float32)
        total = part if total is None else total + part
    return total


def middle_kernel(places, gate_ref, *refs):
    groups, (weight_ref, token_ref, out_ref, tanh_ref) = refs[:-4], refs[-4:]
    gate = jnp.tanh(jnp.full((1, out_ref.shape[1]), gate_ref[0], jnp.float32))
    total = functools.reduce(
        jnp.add, [project(at, groups[2 * i], groups[2 * i + 1], weight_ref) for i, at in enumerate(places)]
    )
    out_ref[...] = token_ref[...].astype(jnp.float32) + gate * total
    tanh_ref[...] = jnp.broadcast_to(gate, tanh_ref.shape)


def mix_kernel(places, own_ref, last_ref, partial_ref, tanh_ref, weight_ref, out_ref):
    total = project(places, own_ref, last_ref, weight_ref)
    out_ref[...] = (partial_ref[...] + tanh_ref[:1, :] * total).astype(jnp.bfloat16)


def kernel_call(kernel, limit, shape, in_specs, args, scratch=()):
    return pl.pallas_call(
        kernel,
        out_shape=shape,
        in_specs=in_specs,
        out_specs=jax.tree.map(lambda _: VMEM, shape),
        scratch_shapes=list(scratch),
        compiler_params=pltpu.CompilerParams(vmem_limit_bytes=limit << 20),
    )(*args)


def body(
    dp,
    mp,
    tokens,
    norm_gain,
    query_weight,
    out_weight,
    gate_scalar,
    image_keys,
    image_values,
    active_image,
    image_slot,
):
    rows = tokens.shape[0]
    arrays, places = gather_wide(tokens, dp)
    keys = [exchange(image_keys, "mp", mp, k) for k in range(1, mp)]
    values = [exchange(image_values, "mp", mp, k) for k in range(1, mp)]

    like = lambda x: jax.ShapeDtypeStruct(x.shape, x.dtype)
    floats = lambda *shape: jax.ShapeDtypeStruct(shape, jnp.float32)
    width = query_weight.shape[1]
    loaded = (tokens, query_weight, image_keys, image_values, norm_gain.reshape(-1, 128), active_image.T, image_slot)
    wanted, stats, own, weight, own_keys, own_values, gain = kernel_call(
        load_kernel,
        2,
        (jax.ShapeDtypeStruct((rows, 128), jnp.int32), floats(2, rows, 128), *map(like, loaded[:5])),
        [VMEM] * EARLY + [HBM] * LOADED,
        (*arrays[:EARLY], *[pltpu.with_memory_space_constraint(x, pltpu.HBM) for x in loaded]),
        [*[pltpu.SMEM(x.shape, x.dtype) for x in loaded[5:]], pltpu.SemaphoreType.DMA((LOADED,))],
    )
    attended = kernel_call(
        functools.partial(attend_kernel, [[0], *places], EARLY + 1, mp),
        16,
        jax.ShapeDtypeStruct((rows, width), jnp.bfloat16),
        [VMEM] * (len(arrays) + 5 + 2 * mp),
        (own[None], *arrays, gain, weight, wanted, stats, own_keys, *keys, own_values, *values),
    )
    heads, places = gather_small(attended, dp)
    pairs = [heads[i] for i in range(1, len(heads) - 1)]
    partial, gate = kernel_call(
        functools.partial(middle_kernel, places[1:-1:2]),
        4,
        (floats(*tokens.shape), floats(8, tokens.shape[1])),
        [SMEM] + [VMEM] * (len(pairs) + 2),
        (gate_scalar, *pairs, out_weight, tokens),
    )
    return kernel_call(
        functools.partial(mix_kernel, places[0]),
        4,
        like(tokens),
        [VMEM] * 5,
        (heads[0], heads[-1], partial, gate, out_weight),
    )


def solution(mesh):
    dp, mp = mesh.shape["dp"], mesh.shape["mp"]
    in_specs = (
        P("mp", "dp"),
        P(),
        P(None, "dp"),
        P(None, "dp"),
        P(),
        P("mp", None, "dp"),
        P("mp", None, "dp"),
        P(),
        P(),
    )

    def step(*args):
        return body(dp, mp, *args)

    return jax.shard_map(step, mesh=mesh, in_specs=in_specs, out_specs=P("mp", "dp"), check_vma=False)
```

time: 41.3 us -> 41.2 us (level)
  waiting for transfers between devices: 12 us -> 13.9 us
  local copies, waits for them, and re-layouts: 1.35 us -> 0.01 us
  Pallas kernels: 5 us -> 4.44 us
    ppermute x18, waiting for transfers between devices: 12 us -> 13.9 us  [exchange(): return lax.ppermute(x, axis, [(i, i ^ mask) for i in range(size)])]
    unnamed x10 -> x4, local copies, waits for them, and re-layouts: 1.35 us -> 0.01 us
    pallas_call x4, Pallas kernels: 5 us -> 4.44 us  [kernel_call(): pl.pallas_call(kernel, out_shape=shape, in_specs=in_specs, out_specs=jax....]
  transfers between devices with their start and end apart: 18 -> 18, of which waited for: 9 -> 10; matrix products, arithmetic and copies ran while one was open for 0% -> 0% of each run, Pallas kernels for 6% -> 5%
where the time goes in v2:
time: 41.2 us; the launch traced here: 41 us
  starting transfers between devices  21.9 us (53%)
  waiting for transfers between devices  13.9 us (34%)
  Pallas kernels  4.44 us (11%)
  between operations  0.73 us (2%)
    ppermute x18, starting transfers between devices, exchange(): return lax.ppermute(x, axis, [(i, i ^ mask) for i in range(size)])  21.9 us
    ppermute x18, waiting for transfers between devices, exchange(): return lax.ppermute(x, axis, [(i, i ^ mask) for i in range(size)])  13.9 us
    pallas_call x4, Pallas kernels, kernel_call(): pl.pallas_call(kernel, out_shape=shape, in_specs=in_specs, out_specs=jax....  4.44 us
  transfers between devices with their start and end apart: 18, of which 10 were waited for; matrix products, arithmetic and copies ran while one was open for 0% of the time, Pallas kernels for 5%

profile of v2, /device:TPU:0, one launch (start us, length us, event | category | flops | bytes accessed | tf_op | source)
XLA Modules:
  0.0 41.0 jit_solution(7361607307824905761)
XLA Ops:
  0.0 4.1 %collective-permute-start.1 = (bf16[64,512]{1,0:T(8,128)(2,1)}, bf16[64,512]{1,0:T(8,128)(2,1)S(1)}, u32[]{:S(2)}, u32[]{:S(2)}) collective-permute-start(bf16[64,512]{1,0:T(8,128)(2,1)} %refs_3_.3), channel_id=1, source_target_pairs={{0,16},{2,18},{4,20},{6,22},{8,24},{10,26},{12,28},{14,30},{16,0},... | collective-permute-start | bytes 196616 | tf_op jit(solution)/shard_map/ppermute | solution.py:29
  4.1 1.3 %collective-permute-start.2 = (bf16[64,512]{1,0:T(8,128)(2,1)}, bf16[64,512]{1,0:T(8,128)(2,1)S(1)}, u32[]{:S(2)}, u32[]{:S(2)}) collective-permute-start(bf16[64,512]{1,0:T(8,128)(2,1)} %refs_3_.3), channel_id=1, source_target_pairs={{0,24},{2,26},{4,28},{6,30},{8,16},{10,18},{12,20},{14,22},{16,8},... | collective-permute-start | bytes 196616 | tf_op jit(solution)/shard_map/ppermute | solution.py:29
  5.4 2.4 %collective-permute-start.3 = (bf16[64,512]{1,0:T(8,128)(2,1)}, bf16[64,512]{1,0:T(8,128)(2,1)S(1)}, u32[]{:S(2)}, u32[]{:S(2)}) collective-permute-start(bf16[64,512]{1,0:T(8,128)(2,1)} %refs_3_.3), channel_id=1, source_target_pairs={{0,6},{2,4},{4,2},{6,0},{8,14},{10,12},{12,10},{14,8},{16,22},{18,... | collective-permute-start | bytes 196616 | tf_op jit(solution)/shard_map/ppermute | solution.py:29
  7.9 0.5 %collective-permute-start.4 = (bf16[64,512]{1,0:T(8,128)(2,1)}, bf16[64,512]{1,0:T(8,128)(2,1)S(1)}, u32[]{:S(2)}, u32[]{:S(2)}) collective-permute-start(bf16[64,512]{1,0:T(8,128)(2,1)} %refs_3_.3), channel_id=1, source_target_pairs={{0,4},{2,6},{4,0},{6,2},{8,12},{10,14},{12,8},{14,10},{16,20},{18,... | collective-permute-start | bytes 196616 | tf_op jit(solution)/shard_map/ppermute | solution.py:29
  8.4 0.5 %collective-permute-start.5 = (bf16[64,512]{1,0:T(8,128)(2,1)}, bf16[64,512]{1,0:T(8,128)(2,1)S(1)}, u32[]{:S(2)}, u32[]{:S(2)}) collective-permute-start(bf16[64,512]{1,0:T(8,128)(2,1)} %refs_3_.3), channel_id=1, source_target_pairs={{0,2},{2,0},{4,6},{6,4},{8,10},{10,8},{12,14},{14,12},{16,18},{18,... | collective-permute-start | bytes 196616 | tf_op jit(solution)/shard_map/ppermute | solution.py:29
  8.9 0.0 collective-permute-done.1
  8.9 1.5 %collective-permute-start = (bf16[64,512]{1,0:T(8,128)(2,1)}, bf16[64,512]{1,0:T(8,128)(2,1)S(1)}, u32[]{:S(2)}, u32[]{:S(2)}) collective-permute-start(bf16[64,512]{1,0:T(8,128)(2,1)} %refs_3_.3), channel_id=1, source_target_pairs={{0,8},{2,10},{4,12},{6,14},{8,0},{10,2},{12,4},{14,6},{16,24},{18,... | collective-permute-start | bytes 196616 | tf_op jit(solution)/shard_map/ppermute | solution.py:29
  10.4 0.1 collective-permute-done.2
  10.4 0.0 collective-permute-start.10
  10.5 0.4 %collective-permute-done.3 = bf16[64,512]{1,0:T(8,128)(2,1)S(1)} collective-permute-done((bf16[64,512]{1,0:T(8,128)(2,1)}, bf16[64,512]{1,0:T(8,128)(2,1)S(1)}, u32[]{:S(2)}, u32[]{:S(2)}) %collective-permute-start.3) | collective-permute-done | bytes 65568 | tf_op jit(solution)/shard_map/ppermute | solution.py:29
  10.9 0.2 collective-permute-start.11
  11.0 1.3 %collective-permute-done.4 = bf16[64,512]{1,0:T(8,128)(2,1)S(1)} collective-permute-done((bf16[64,512]{1,0:T(8,128)(2,1)}, bf16[64,512]{1,0:T(8,128)(2,1)S(1)}, u32[]{:S(2)}, u32[]{:S(2)}) %collective-permute-start.4) | collective-permute-done | bytes 65568 | tf_op jit(solution)/shard_map/ppermute | solution.py:29
  12.3 1.2 %collective-permute-start.6 = (bf16[2,64,512]{2,1,0:T(8,128)(2,1)S(1)}, bf16[2,64,512]{2,1,0:T(8,128)(2,1)S(1)}, u32[]{:S(2)}, u32[]{:S(2)}) collective-permute-start(bf16[2,64,512]{2,1,0:T(8,128)(2,1)S(1)} %pad_maximum_fusion.1.refs_1_.refs_2_), channel_id=1, source_target_pairs={{0,6},{2,4},{4,2},{6,0},{8,14},{10,12},{12,10},{14,8},{16,22},{18,... | collective-permute-start | bytes 393224 | tf_op jit(solution)/shard_map/ppermute | solution.py:29
  13.5 0.0 collective-permute-done.5
  13.6 1.1 %collective-permute-start.9 = (bf16[3,64,512]{2,1,0:T(8,128)(2,1)S(1)}, bf16[3,64,512]{2,1,0:T(8,128)(2,1)S(1)}, u32[]{:S(2)}, u32[]{:S(2)}) collective-permute-start(bf16[3,64,512]{2,1,0:T(8,128)(2,1)S(1)} %pad_maximum_fusion.refs_2_.refs_3_), channel_id=1, source_target_pairs={{0,8},{2,10},{4,12},{6,14},{8,0},{10,2},{12,4},{14,6},{16,24},{18,... | collective-permute-start | bytes 589832 | tf_op jit(solution)/shard_map/ppermute | solution.py:29
  14.7 0.0 collective-permute-done
  14.7 0.5 %collective-permute-start.7 = (bf16[2,64,512]{2,1,0:T(8,128)(2,1)S(1)}, bf16[2,64,512]{2,1,0:T(8,128)(2,1)S(1)}, u32[]{:S(2)}, u32[]{:S(2)}) collective-permute-start(bf16[2,64,512]{2,1,0:T(8,128)(2,1)S(1)} %pad_maximum_fusion.1.refs_1_.refs_2_), channel_id=1, source_target_pairs={{0,4},{2,6},{4,0},{6,2},{8,12},{10,14},{12,8},{14,10},{16,20},{18,... | collective-permute-start | bytes 393224 | tf_op jit(solution)/shard_map/ppermute | solution.py:29
  15.2 3.1 %collective-permute-done.6.refs_4_ = bf16[2,64,512]{2,1,0:T(8,128)(2,1)S(1)} collective-permute-done((bf16[2,64,512]{2,1,0:T(8,128)(2,1)S(1)}, bf16[2,64,512]{2,1,0:T(8,128)(2,1)S(1)}, u32[]{:S(2)}, u32[]{:S(2)}) %collective-permute-start.6) | collective-permute-done | bytes 131104 | tf_op jit(solution)/shard_map/ppermute | solution.py:29
  18.3 1.5 %collective-permute-start.8 = (bf16[2,64,512]{2,1,0:T(8,128)(2,1)S(1)}, bf16[2,64,512]{2,1,0:T(8,128)(2,1)S(1)}, u32[]{:S(2)}, u32[]{:S(2)}) collective-permute-start(bf16[2,64,512]{2,1,0:T(8,128)(2,1)S(1)} %pad_maximum_fusion.1.refs_1_.refs_2_), channel_id=1, source_target_pairs={{0,2},{2,0},{4,6},{6,4},{8,10},{10,8},{12,14},{14,12},{16,18},{18,... | collective-permute-start | bytes 393224 | tf_op jit(solution)/shard_map/ppermute | solution.py:29
  19.8 1.8 %shard_map.91 = (s32[64,128]{1,0:T(8,128)S(1)}, f32[2,64,128]{2,1,0:T(8,128)S(1)}, bf16[64,512]{1,0:T(8,128)(2,1)S(1)}, bf16[8192,128]{1,0:T(8,128)(2,1)S(1)}, b...) custom-call(bf16[1,64,512]{2,1,0:T(8,128)(2,1)S(1)} %bitcast.13, ...), custom_call_target="tpu_custom_call" | custom-call | tf_op jit(solution)/shard_map/pallas_call | solution.py:211
  21.6 0.0 collective-permute-done.7.refs_5_
  21.6 1.7 %collective-permute-done.8.refs_6_ = bf16[2,64,512]{2,1,0:T(8,128)(2,1)S(1)} collective-permute-done((bf16[2,64,512]{2,1,0:T(8,128)(2,1)S(1)}, bf16[2,64,512]{2,1,0:T(8,128)(2,1)S(1)}, u32[]{:S(2)}, u32[]{:S(2)}) %collective-permute-start.8) | collective-permute-done | bytes 131104 | tf_op jit(solution)/shard_map/ppermute | solution.py:29
  23.3 0.0 collective-permute-done.9.refs_7_
  23.3 0.0 collective-permute-done.10.refs_13_
  23.3 0.0 collective-permute-done.11.refs_15_
  23.3 0.0 copy-start
  23.3 0.0 copy-start.1
  23.3 1.5 %shard_map.92 = bf16[64,128]{1,0:T(8,128)(2,1)S(1)} custom-call(bf16[1,64,512]{2,1,0:T(8,128)(2,1)S(1)} %bitcast.15, bf16[1,64,512]{2,1,0:T(8,128)(2,1)S(1)} %bitcast.14, bf16[2,64,512]{2,1,0:T(8,128)(2,1)S(1)} %pad_maximum_fusion.1.refs_1_.refs_2_, bf16[3,64,512]{2,1,0:T(8,128)(2,1)S(1)} %pad_maximum_fusion.refs_2_.refs_3_, ...), custom_call_target="tpu_custom_call" | custom-call | tf_op jit(solution)/shard_map/pallas_call | solution.py:211
  24.8 2.5 %collective-permute-start.12 = (bf16[64,128]{1,0:T(8,128)(2,1)S(1)}, bf16[64,128]{1,0:T(8,128)(2,1)S(1)}, u32[]{:S(2)}, u32[]{:S(2)}) collective-permute-start(bf16[64,128]{1,0:T(8,128)(2,1)S(1)} %shard_map.92), channel_id=1, source_target_pairs={{0,16},{2,18},{4,20},{6,22},{8,24},{10,26},{12,28},{14,30},{16,0},... | collective-permute-start | bytes 49160 | tf_op jit(solution)/shard_map/ppermute | solution.py:29
  27.3 0.1 collective-permute-start.13
  27.4 1.0 %collective-permute-start.14 = (bf16[64,128]{1,0:T(8,128)(2,1)S(1)}, bf16[64,128]{1,0:T(8,128)(2,1)S(1)}, u32[]{:S(2)}, u32[]{:S(2)}) collective-permute-start(bf16[64,128]{1,0:T(8,128)(2,1)S(1)} %shard_map.92), channel_id=1, source_target_pairs={{0,8},{2,10},{4,12},{6,14},{8,0},{10,2},{12,4},{14,6},{16,24},{18,... | collective-permute-start | bytes 49160 | tf_op jit(solution)/shard_map/ppermute | solution.py:29
  28.3 1.3 %collective-permute-done.12 = bf16[64,128]{1,0:T(8,128)(2,1)S(1)} collective-permute-done((bf16[64,128]{1,0:T(8,128)(2,1)S(1)}, bf16[64,128]{1,0:T(8,128)(2,1)S(1)}, u32[]{:S(2)}, u32[]{:S(2)}) %collective-permute-start.12) | collective-permute-done | bytes 16416 | tf_op jit(solution)/shard_map/ppermute | solution.py:29
  29.7 3.2 %collective-permute-done.13 = bf16[64,128]{1,0:T(8,128)(2,1)S(1)} collective-permute-done((bf16[64,128]{1,0:T(8,128)(2,1)S(1)}, bf16[64,128]{1,0:T(8,128)(2,1)S(1)}, u32[]{:S(2)}, u32[]{:S(2)}) %collective-permute-start.13) | collective-permute-done | bytes 16416 | tf_op jit(solution)/shard_map/ppermute | solution.py:29
  32.8 0.0 collective-permute-done.14
  32.8 2.5 %collective-permute-start.16 = (bf16[4,64,128]{2,1,0:T(8,128)(2,1)S(1)}, bf16[4,64,128]{2,1,0:T(8,128)(2,1)S(1)}, u32[]{:S(2)}, u32[]{:S(2)}) collective-permute-start(bf16[4,64,128]{2,1,0:T(8,128)(2,1)S(1)} %pad_maximum_fusion.2.own_ref), channel_id=1, source_target_pairs={{0,6},{2,4},{4,2},{6,0},{8,14},{10,12},{12,10},{14,8},{16,22},{18,... | collective-permute-start | bytes 196616 | tf_op jit(solution)/shard_map/ppermute | solution.py:29
  35.3 0.5 %collective-permute-start.17 = (bf16[4,64,128]{2,1,0:T(8,128)(2,1)S(1)}, bf16[4,64,128]{2,1,0:T(8,128)(2,1)S(1)}, u32[]{:S(2)}, u32[]{:S(2)}) collective-permute-start(bf16[4,64,128]{2,1,0:T(8,128)(2,1)S(1)} %pad_maximum_fusion.2.own_ref), channel_id=1, source_target_pairs={{0,4},{2,6},{4,0},{6,2},{8,12},{10,14},{12,8},{14,10},{16,20},{18,... | collective-permute-start | bytes 196616 | tf_op jit(solution)/shard_map/ppermute | solution.py:29
  35.9 0.5 %collective-permute-start.15 = (bf16[4,64,128]{2,1,0:T(8,128)(2,1)S(1)}, bf16[4,64,128]{2,1,0:T(8,128)(2,1)S(1)}, u32[]{:S(2)}, u32[]{:S(2)}) collective-permute-start(bf16[4,64,128]{2,1,0:T(8,128)(2,1)S(1)} %pad_maximum_fusion.2.own_ref), channel_id=1, source_target_pairs={{0,2},{2,0},{4,6},{6,4},{8,10},{10,8},{12,14},{14,12},{16,18},{18,... | collective-permute-start | bytes 196616 | tf_op jit(solution)/shard_map/ppermute | solution.py:29
  37.0 1.0 %collective-permute-done.16.refs_0_ = bf16[4,64,128]{2,1,0:T(8,128)(2,1)S(1)} collective-permute-done((bf16[4,64,128]{2,1,0:T(8,128)(2,1)S(1)}, bf16[4,64,128]{2,1,0:T(8,128)(2,1)S(1)}, u32[]{:S(2)}, u32[]{:S(2)}) %collective-permute-start.16) | collective-permute-done | bytes 65568 | tf_op jit(solution)/shard_map/ppermute | solution.py:29
  38.1 1.5 %collective-permute-done.17.refs_1_ = bf16[4,64,128]{2,1,0:T(8,128)(2,1)S(1)} collective-permute-done((bf16[4,64,128]{2,1,0:T(8,128)(2,1)S(1)}, bf16[4,64,128]{2,1,0:T(8,128)(2,1)S(1)}, u32[]{:S(2)}, u32[]{:S(2)}) %collective-permute-start.17) | collective-permute-done | bytes 65568 | tf_op jit(solution)/shard_map/ppermute | solution.py:29
  39.6 0.0 copy-done
  39.6 0.0 copy-done.1
  39.6 0.3 shard_map.93
  39.9 0.2 collective-permute-done.15.last_ref
  40.1 0.9 %shard_map.94 = bf16[64,512]{1,0:T(8,128)(2,1)} custom-call(bf16[4,64,128]{2,1,0:T(8,128)(2,1)S(1)} %pad_maximum_fusion.2.own_ref, bf16[4,64,128]{2,1,0:T(8,128)(2,1)S(1)} %collective-permute-done.15.last_ref, f32[64,512]{1,0:T(8,128)S(1)} %get-tuple-element.21.partial_ref, f32[8,512]{1,0:T(8,128)S(1)} %get-tuple-element.22.tanh_ref, ...), custom_call_target="tpu_custom_call" | custom-call | tf_op jit(solution)/shard_map/pallas_call | solution.py:211
  (3 shorter events, 0.0 us)
Async XLA Ops:
  0.0 8.9 %collective-permute-start.1 = (bf16[64,512]{1,0:T(8,128)(2,1)}, bf16[64,512]{1,0:T(8,128)(2,1)S(1)}, u32[]{:S(2)}, u32[]{:S(2)}) collective-permute-start(bf16[64,512]{1,0:T(8,128)(2,1)} %refs_3_.3), channel_id=1, source_target_pairs={{0,16},{2,18},{4,20},{6,22},{8,24},{10,26},{12,28},{14,30},{16,0},... | collective-permute-start | bytes 196616 | tf_op jit(solution)/shard_map/ppermute | solution.py:29
  4.1 6.4 %collective-permute-start.2 = (bf16[64,512]{1,0:T(8,128)(2,1)}, bf16[64,512]{1,0:T(8,128)(2,1)S(1)}, u32[]{:S(2)}, u32[]{:S(2)}) collective-permute-start(bf16[64,512]{1,0:T(8,128)(2,1)} %refs_3_.3), channel_id=1, source_target_pairs={{0,24},{2,26},{4,28},{6,30},{8,16},{10,18},{12,20},{14,22},{16,8},... | collective-permute-start | bytes 196616 | tf_op jit(solution)/shard_map/ppermute | solution.py:29
  5.4 5.5 %collective-permute-start.3 = (bf16[64,512]{1,0:T(8,128)(2,1)}, bf16[64,512]{1,0:T(8,128)(2,1)S(1)}, u32[]{:S(2)}, u32[]{:S(2)}) collective-permute-start(bf16[64,512]{1,0:T(8,128)(2,1)} %refs_3_.3), channel_id=1, source_target_pairs={{0,6},{2,4},{4,2},{6,0},{8,14},{10,12},{12,10},{14,8},{16,22},{18,... | collective-permute-start | bytes 196616 | tf_op jit(solution)/shard_map/ppermute | solution.py:29
  7.9 4.5 %collective-permute-start.4 = (bf16[64,512]{1,0:T(8,128)(2,1)}, bf16[64,512]{1,0:T(8,128)(2,1)S(1)}, u32[]{:S(2)}, u32[]{:S(2)}) collective-permute-start(bf16[64,512]{1,0:T(8,128)(2,1)} %refs_3_.3), channel_id=1, source_target_pairs={{0,4},{2,6},{4,0},{6,2},{8,12},{10,14},{12,8},{14,10},{16,20},{18,... | collective-permute-start | bytes 196616 | tf_op jit(solution)/shard_map/ppermute | solution.py:29
  8.4 5.2 %collective-permute-start.5 = (bf16[64,512]{1,0:T(8,128)(2,1)}, bf16[64,512]{1,0:T(8,128)(2,1)S(1)}, u32[]{:S(2)}, u32[]{:S(2)}) collective-permute-start(bf16[64,512]{1,0:T(8,128)(2,1)} %refs_3_.3), channel_id=1, source_target_pairs={{0,2},{2,0},{4,6},{6,4},{8,10},{10,8},{12,14},{14,12},{16,18},{18,... | collective-permute-start | bytes 196616 | tf_op jit(solution)/shard_map/ppermute | solution.py:29
  8.9 5.8 %collective-permute-start = (bf16[64,512]{1,0:T(8,128)(2,1)}, bf16[64,512]{1,0:T(8,128)(2,1)S(1)}, u32[]{:S(2)}, u32[]{:S(2)}) collective-permute-start(bf16[64,512]{1,0:T(8,128)(2,1)} %refs_3_.3), channel_id=1, source_target_pairs={{0,8},{2,10},{4,12},{6,14},{8,0},{10,2},{12,4},{14,6},{16,24},{18,... | collective-permute-start | bytes 196616 | tf_op jit(solution)/shard_map/ppermute | solution.py:29
  10.4 12.8 %collective-permute-start.10 = (bf16[16,64,128]{2,1,0:T(8,128)(2,1)}, bf16[16,64,128]{2,1,0:T(8,128)(2,1)S(1)}, u32[]{:S(2)}, u32[]{:S(2)}) collective-permute-start(bf16[16,64,128]{2,1,0:T(8,128)(2,1)} %refs_5_.1), channel_id=1, source_target_pairs={{0,1},{1,0},{2,3},{3,2},{4,5},{5,4},{6,7},{7,6},{8,9},{9,8},{10,11... | collective-permute-start | bytes 786440 | tf_op jit(solution)/shard_map/ppermute | solution.py:29
  10.9 12.4 %collective-permute-start.11 = (bf16[16,64,128]{2,1,0:T(8,128)(2,1)}, bf16[16,64,128]{2,1,0:T(8,128)(2,1)S(1)}, u32[]{:S(2)}, u32[]{:S(2)}) collective-permute-start(bf16[16,64,128]{2,1,0:T(8,128)(2,1)} %refs_6_.1), channel_id=1, source_target_pairs={{0,1},{1,0},{2,3},{3,2},{4,5},{5,4},{6,7},{7,6},{8,9},{9,8},{10,11... | collective-permute-start | bytes 786440 | tf_op jit(solution)/shard_map/ppermute | solution.py:29
  12.3 6.0 %collective-permute-start.6 = (bf16[2,64,512]{2,1,0:T(8,128)(2,1)S(1)}, bf16[2,64,512]{2,1,0:T(8,128)(2,1)S(1)}, u32[]{:S(2)}, u32[]{:S(2)}) collective-permute-start(bf16[2,64,512]{2,1,0:T(8,128)(2,1)S(1)} %pad_maximum_fusion.1.refs_1_.refs_2_), channel_id=1, source_target_pairs={{0,6},{2,4},{4,2},{6,0},{8,14},{10,12},{12,10},{14,8},{16,22},{18,... | collective-permute-start | bytes 393224 | tf_op jit(solution)/shard_map/ppermute | solution.py:29
  13.6 9.7 %collective-permute-start.9 = (bf16[3,64,512]{2,1,0:T(8,128)(2,1)S(1)}, bf16[3,64,512]{2,1,0:T(8,128)(2,1)S(1)}, u32[]{:S(2)}, u32[]{:S(2)}) collective-permute-start(bf16[3,64,512]{2,1,0:T(8,128)(2,1)S(1)} %pad_maximum_fusion.refs_2_.refs_3_), channel_id=1, source_target_pairs={{0,8},{2,10},{4,12},{6,14},{8,0},{10,2},{12,4},{14,6},{16,24},{18,... | collective-permute-start | bytes 589832 | tf_op jit(solution)/shard_map/ppermute | solution.py:29
  14.7 6.9 %collective-permute-start.7 = (bf16[2,64,512]{2,1,0:T(8,128)(2,1)S(1)}, bf16[2,64,512]{2,1,0:T(8,128)(2,1)S(1)}, u32[]{:S(2)}, u32[]{:S(2)}) collective-permute-start(bf16[2,64,512]{2,1,0:T(8,128)(2,1)S(1)} %pad_maximum_fusion.1.refs_1_.refs_2_), channel_id=1, source_target_pairs={{0,4},{2,6},{4,0},{6,2},{8,12},{10,14},{12,8},{14,10},{16,20},{18,... | collective-permute-start | bytes 393224 | tf_op jit(solution)/shard_map/ppermute | solution.py:29
  18.3 5.0 %collective-permute-start.8 = (bf16[2,64,512]{2,1,0:T(8,128)(2,1)S(1)}, bf16[2,64,512]{2,1,0:T(8,128)(2,1)S(1)}, u32[]{:S(2)}, u32[]{:S(2)}) collective-permute-start(bf16[2,64,512]{2,1,0:T(8,128)(2,1)S(1)} %pad_maximum_fusion.1.refs_1_.refs_2_), channel_id=1, source_target_pairs={{0,2},{2,0},{4,6},{6,4},{8,10},{10,8},{12,14},{14,12},{16,18},{18,... | collective-permute-start | bytes 393224 | tf_op jit(solution)/shard_map/ppermute | solution.py:29
  23.3 16.3 %copy-start = (bf16[2048,512]{1,0:T(8,128)(2,1)S(1)}, bf16[2048,512]{1,0:T(8,128)(2,1)}, u32[]{:S(2)}) copy-start(bf16[2048,512]{1,0:T(8,128)(2,1)} %weight_ref.1) | copy-start | bytes 6291460
  23.3 16.3 %copy-start.1 = (bf16[64,512]{1,0:T(8,128)(2,1)S(1)}, bf16[64,512]{1,0:T(8,128)(2,1)}, u32[]{:S(2)}) copy-start(bf16[64,512]{1,0:T(8,128)(2,1)} %refs_3_.3) | copy-start | bytes 196612
  24.8 4.9 %collective-permute-start.12 = (bf16[64,128]{1,0:T(8,128)(2,1)S(1)}, bf16[64,128]{1,0:T(8,128)(2,1)S(1)}, u32[]{:S(2)}, u32[]{:S(2)}) collective-permute-start(bf16[64,128]{1,0:T(8,128)(2,1)S(1)} %shard_map.92), channel_id=1, source_target_pairs={{0,16},{2,18},{4,20},{6,22},{8,24},{10,26},{12,28},{14,30},{16,0},... | collective-permute-start | bytes 49160 | tf_op jit(solution)/shard_map/ppermute | solution.py:29
  27.3 5.5 %collective-permute-start.13 = (bf16[64,128]{1,0:T(8,128)(2,1)S(1)}, bf16[64,128]{1,0:T(8,128)(2,1)S(1)}, u32[]{:S(2)}, u32[]{:S(2)}) collective-permute-start(bf16[64,128]{1,0:T(8,128)(2,1)S(1)} %shard_map.92), channel_id=1, source_target_pairs={{0,24},{2,26},{4,28},{6,30},{8,16},{10,18},{12,20},{14,22},{16,8},... | collective-permute-start | bytes 49160 | tf_op jit(solution)/shard_map/ppermute | solution.py:29
  27.4 5.4 %collective-permute-start.14 = (bf16[64,128]{1,0:T(8,128)(2,1)S(1)}, bf16[64,128]{1,0:T(8,128)(2,1)S(1)}, u32[]{:S(2)}, u32[]{:S(2)}) collective-permute-start(bf16[64,128]{1,0:T(8,128)(2,1)S(1)} %shard_map.92), channel_id=1, source_target_pairs={{0,8},{2,10},{4,12},{6,14},{8,0},{10,2},{12,4},{14,6},{16,24},{18,... | collective-permute-start | bytes 49160 | tf_op jit(solution)/shard_map/ppermute | solution.py:29
  32.8 5.2 %collective-permute-start.16 = (bf16[4,64,128]{2,1,0:T(8,128)(2,1)S(1)}, bf16[4,64,128]{2,1,0:T(8,128)(2,1)S(1)}, u32[]{:S(2)}, u32[]{:S(2)}) collective-permute-start(bf16[4,64,128]{2,1,0:T(8,128)(2,1)S(1)} %pad_maximum_fusion.2.own_ref), channel_id=1, source_target_pairs={{0,6},{2,4},{4,2},{6,0},{8,14},{10,12},{12,10},{14,8},{16,22},{18,... | collective-permute-start | bytes 196616 | tf_op jit(solution)/shard_map/ppermute | solution.py:29
  35.3 4.3 %collective-permute-start.17 = (bf16[4,64,128]{2,1,0:T(8,128)(2,1)S(1)}, bf16[4,64,128]{2,1,0:T(8,128)(2,1)S(1)}, u32[]{:S(2)}, u32[]{:S(2)}) collective-permute-start(bf16[4,64,128]{2,1,0:T(8,128)(2,1)S(1)} %pad_maximum_fusion.2.own_ref), channel_id=1, source_target_pairs={{0,4},{2,6},{4,0},{6,2},{8,12},{10,14},{12,8},{14,10},{16,20},{18,... | collective-permute-start | bytes 196616 | tf_op jit(solution)/shard_map/ppermute | solution.py:29
  35.9 4.3 %collective-permute-start.15 = (bf16[4,64,128]{2,1,0:T(8,128)(2,1)S(1)}, bf16[4,64,128]{2,1,0:T(8,128)(2,1)S(1)}, u32[]{:S(2)}, u32[]{:S(2)}) collective-permute-start(bf16[4,64,128]{2,1,0:T(8,128)(2,1)S(1)} %pad_maximum_fusion.2.own_ref), channel_id=1, source_target_pairs={{0,2},{2,0},{4,6},{6,4},{8,10},{10,8},{12,14},{14,12},{16,18},{18,... | collective-permute-start | bytes 196616 | tf_op jit(solution)/shard_map/ppermute | solution.py:29

commit v3 on v2

--- a/solution.py
+++ b/solution.py
@@ -105,6 +105,30 @@
         copy.wait()
 
 
+def deviations(tiles, shift, total, squares):
+    lane = shift.shape[1]
+
+    def add(c, carry):
+        total, squares = carry
+        for tile in tiles:
+            moved = tile[:, pl.ds(pl.multiple_of(c * lane, lane), lane)].astype(jnp.float32) - shift
+            total += moved
+            squares += moved * moved
+        return total, squares
+
+    return lax.fori_loop(0, tiles[0].shape[1] // lane, add, (total, squares))
+
+
+def lead_kernel(*refs):
+    groups, (stats_ref, sums_ref) = refs[:-2], refs[-2:]
+    tiles = [g.at[i] for g in groups for i in range(g.shape[0])]
+    shift = stats_ref[0]
+    total, squares = deviations(tiles, shift, jnp.zeros_like(shift), stats_ref[1])
+    sums_ref[0] = shift
+    sums_ref[1] = squares
+    sums_ref[2] = total
+
+
 def attend_kernel(places, early, mp, *refs):
     tiles = len(places)
     groups, refs = refs[:tiles], refs[tiles:]
@@ -115,19 +139,11 @@
     lane = wanted_ref.shape[1]
     chunks = wide // lane
     model = weight_ref.shape[0]
-    late = [g.at[i] for g in groups[early:] for i in range(g.shape[0])]
+    late = [g.at[i] for g in groups[early:-1] for i in range(g.shape[0])]
 
     shift = stats_ref[0]
 
-    def add(c, carry):
-        total, squares = carry
-        for tile in late:
-            moved = tile[:, pl.ds(pl.multiple_of(c * lane, lane), lane)].astype(jnp.float32) - shift
-            total += moved
-            squares += moved * moved
-        return total, squares
-
-    total, squares = lax.fori_loop(0, chunks, add, (jnp.zeros((rows, lane), jnp.float32), stats_ref[1]))
+    total, squares = deviations(late, shift, stats_ref[2], stats_ref[1])
     offset = jnp.sum(total, axis=1, keepdims=True) * (1.0 / model)
     variance = jnp.sum(squares, axis=1, keepdims=True) * (1.0 / model) - offset * offset
     average = shift + offset
@@ -248,8 +264,12 @@
         (*arrays[:EARLY], *[pltpu.with_memory_space_constraint(x, pltpu.HBM) for x in loaded]),
         [*[pltpu.SMEM(x.shape, x.dtype) for x in loaded[5:]], pltpu.SemaphoreType.DMA((LOADED,))],
     )
+    ahead = [*range(EARLY, len(arrays) - 3), len(arrays) - 1]
+    stats = kernel_call(
+        lead_kernel, 2, floats(3, rows, 128), [VMEM] * (len(ahead) + 1), (*[arrays[i] for i in ahead], stats)
+    )
     attended = kernel_call(
-        functools.partial(attend_kernel, [[0], *places], EARLY + 1, mp),
+        functools.partial(attend_kernel, [[0], *places], len(arrays) - 2, mp),
         16,
         jax.ShapeDtypeStruct((rows, width), jnp.bfloat16),
         [VMEM] * (len(arrays) + 5 + 2 * mp),

time: 41.2 us -> 44.2 us (1.073)
  waiting for transfers between devices: 13.9 us -> 17.2 us
    ppermute x18, waiting for transfers between devices: 13.9 us -> 17.2 us  [exchange(): return lax.ppermute(x, axis, [(i, i ^ mask) for i in range(size)])]
    pallas_call x4 -> x5, Pallas kernels: 4.44 us -> 4.47 us  [kernel_call(): pl.pallas_call(kernel, out_shape=shape, in_specs=in_specs, out_specs=jax....]
where the time goes in v3:
time: 44.2 us; the launch traced here: 44 us
  starting transfers between devices  21.6 us (49%)
  waiting for transfers between devices  17.2 us (39%)
  Pallas kernels  4.47 us (10%)
  between operations  0.73 us (2%)
    ppermute x18, starting transfers between devices, exchange(): return lax.ppermute(x, axis, [(i, i ^ mask) for i in range(size)])  21.6 us
    ppermute x18, waiting for transfers between devices, exchange(): return lax.ppermute(x, axis, [(i, i ^ mask) for i in range(size)])  17.2 us
    pallas_call x5, Pallas kernels, kernel_call(): pl.pallas_call(kernel, out_shape=shape, in_specs=in_specs, out_specs=jax....  4.47 us
  transfers between devices with their start and end apart: 18, of which 10 were waited for; matrix products, arithmetic and copies ran while one was open for 0% of the time, Pallas kernels for 5%

profile of v3, /device:TPU:0, one launch (start us, length us, event | category | flops | bytes accessed | tf_op | source)
XLA Modules:
  0.0 44.0 jit_solution(878741465001990248)
XLA Ops:
  0.0 4.1 %collective-permute-start.1 = (bf16[64,512]{1,0:T(8,128)(2,1)}, bf16[64,512]{1,0:T(8,128)(2,1)S(1)}, u32[]{:S(2)}, u32[]{:S(2)}) collective-permute-start(bf16[64,512]{1,0:T(8,128)(2,1)} %refs_3_.3), channel_id=1, source_target_pairs={{0,16},{2,18},{4,20},{6,22},{8,24},{10,26},{12,28},{14,30},{16,0},... | collective-permute-start | bytes 196616 | tf_op jit(solution)/shard_map/ppermute | solution.py:29
  4.1 1.3 %collective-permute-start.2 = (bf16[64,512]{1,0:T(8,128)(2,1)}, bf16[64,512]{1,0:T(8,128)(2,1)S(1)}, u32[]{:S(2)}, u32[]{:S(2)}) collective-permute-start(bf16[64,512]{1,0:T(8,128)(2,1)} %refs_3_.3), channel_id=1, source_target_pairs={{0,24},{2,26},{4,28},{6,30},{8,16},{10,18},{12,20},{14,22},{16,8},... | collective-permute-start | bytes 196616 | tf_op jit(solution)/shard_map/ppermute | solution.py:29
  5.4 2.4 %collective-permute-start.3 = (bf16[64,512]{1,0:T(8,128)(2,1)}, bf16[64,512]{1,0:T(8,128)(2,1)S(1)}, u32[]{:S(2)}, u32[]{:S(2)}) collective-permute-start(bf16[64,512]{1,0:T(8,128)(2,1)} %refs_3_.3), channel_id=1, source_target_pairs={{0,6},{2,4},{4,2},{6,0},{8,14},{10,12},{12,10},{14,8},{16,22},{18,... | collective-permute-start | bytes 196616 | tf_op jit(solution)/shard_map/ppermute | solution.py:29
  7.9 0.5 %collective-permute-start.4 = (bf16[64,512]{1,0:T(8,128)(2,1)}, bf16[64,512]{1,0:T(8,128)(2,1)S(1)}, u32[]{:S(2)}, u32[]{:S(2)}) collective-permute-start(bf16[64,512]{1,0:T(8,128)(2,1)} %refs_3_.3), channel_id=1, source_target_pairs={{0,4},{2,6},{4,0},{6,2},{8,12},{10,14},{12,8},{14,10},{16,20},{18,... | collective-permute-start | bytes 196616 | tf_op jit(solution)/shard_map/ppermute | solution.py:29
  8.4 0.5 %collective-permute-start.5 = (bf16[64,512]{1,0:T(8,128)(2,1)}, bf16[64,512]{1,0:T(8,128)(2,1)S(1)}, u32[]{:S(2)}, u32[]{:S(2)}) collective-permute-start(bf16[64,512]{1,0:T(8,128)(2,1)} %refs_3_.3), channel_id=1, source_target_pairs={{0,2},{2,0},{4,6},{6,4},{8,10},{10,8},{12,14},{14,12},{16,18},{18,... | collective-permute-start | bytes 196616 | tf_op jit(solution)/shard_map/ppermute | solution.py:29
  8.9 0.0 collective-permute-done.1
  8.9 0.0 collective-permute-start.10
  8.9 1.5 %collective-permute-done.2 = bf16[64,512]{1,0:T(8,128)(2,1)S(1)} collective-permute-done((bf16[64,512]{1,0:T(8,128)(2,1)}, bf16[64,512]{1,0:T(8,128)(2,1)S(1)}, u32[]{:S(2)}, u32[]{:S(2)}) %collective-permute-start.2) | collective-permute-done | bytes 65568 | tf_op jit(solution)/shard_map/ppermute | solution.py:29
  10.4 0.0 collective-permute-start.11
  10.5 0.4 collective-permute-done.3
  10.9 2.4 %collective-permute-start.6 = (bf16[2,64,512]{2,1,0:T(8,128)(2,1)S(1)}, bf16[2,64,512]{2,1,0:T(8,128)(2,1)S(1)}, u32[]{:S(2)}, u32[]{:S(2)}) collective-permute-start(bf16[2,64,512]{2,1,0:T(8,128)(2,1)S(1)} %pad_maximum_fusion.1.refs_1_.refs_2_), channel_id=1, source_target_pairs={{0,6},{2,4},{4,2},{6,0},{8,14},{10,12},{12,10},{14,8},{16,22},{18,... | collective-permute-start | bytes 393224 | tf_op jit(solution)/shard_map/ppermute | solution.py:29
  13.3 0.0 collective-permute-done.4
  13.3 0.0 collective-permute-done.5
  13.4 0.8 %collective-permute-start.9 = (bf16[3,64,512]{2,1,0:T(8,128)(2,1)S(1)}, bf16[3,64,512]{2,1,0:T(8,128)(2,1)S(1)}, u32[]{:S(2)}, u32[]{:S(2)}) collective-permute-start(bf16[3,64,512]{2,1,0:T(8,128)(2,1)S(1)} %pad_maximum_fusion.refs_2_.refs_3_), channel_id=1, source_target_pairs={{0,8},{2,10},{4,12},{6,14},{8,0},{10,2},{12,4},{14,6},{16,24},{18,... | collective-permute-start | bytes 589832 | tf_op jit(solution)/shard_map/ppermute | solution.py:29
  14.2 1.3 %collective-permute-start = (bf16[64,512]{1,0:T(8,128)(2,1)}, bf16[64,512]{1,0:T(8,128)(2,1)S(1)}, u32[]{:S(2)}, u32[]{:S(2)}) collective-permute-start(bf16[64,512]{1,0:T(8,128)(2,1)} %refs_3_.3), channel_id=1, source_target_pairs={{0,8},{2,10},{4,12},{6,14},{8,0},{10,2},{12,4},{14,6},{16,24},{18,... | collective-permute-start | bytes 196616 | tf_op jit(solution)/shard_map/ppermute | solution.py:29
  15.5 6.1 %collective-permute-done = bf16[64,512]{1,0:T(8,128)(2,1)S(1)} collective-permute-done((bf16[64,512]{1,0:T(8,128)(2,1)}, bf16[64,512]{1,0:T(8,128)(2,1)S(1)}, u32[]{:S(2)}, u32[]{:S(2)}) %collective-permute-start) | collective-permute-done | bytes 65568 | tf_op jit(solution)/shard_map/ppermute | solution.py:29
  21.5 0.5 %collective-permute-start.7 = (bf16[2,64,512]{2,1,0:T(8,128)(2,1)S(1)}, bf16[2,64,512]{2,1,0:T(8,128)(2,1)S(1)}, u32[]{:S(2)}, u32[]{:S(2)}) collective-permute-start(bf16[2,64,512]{2,1,0:T(8,128)(2,1)S(1)} %pad_maximum_fusion.1.refs_1_.refs_2_), channel_id=1, source_target_pairs={{0,4},{2,6},{4,0},{6,2},{8,12},{10,14},{12,8},{14,10},{16,20},{18,... | collective-permute-start | bytes 393224 | tf_op jit(solution)/shard_map/ppermute | solution.py:29
  22.0 0.0 collective-permute-done.6.refs_0_.refs_4_
  22.0 0.5 %collective-permute-start.8 = (bf16[2,64,512]{2,1,0:T(8,128)(2,1)S(1)}, bf16[2,64,512]{2,1,0:T(8,128)(2,1)S(1)}, u32[]{:S(2)}, u32[]{:S(2)}) collective-permute-start(bf16[2,64,512]{2,1,0:T(8,128)(2,1)S(1)} %pad_maximum_fusion.1.refs_1_.refs_2_), channel_id=1, source_target_pairs={{0,2},{2,0},{4,6},{6,4},{8,10},{10,8},{12,14},{14,12},{16,18},{18,... | collective-permute-start | bytes 393224 | tf_op jit(solution)/shard_map/ppermute | solution.py:29
  22.6 1.8 %shard_map.91 = (s32[64,128]{1,0:T(8,128)S(1)}, f32[2,64,128]{2,1,0:T(8,128)S(1)}, bf16[64,512]{1,0:T(8,128)(2,1)S(1)}, bf16[8192,128]{1,0:T(8,128)(2,1)S(1)}, b...) custom-call(bf16[1,64,512]{2,1,0:T(8,128)(2,1)S(1)} %bitcast.13, ...), custom_call_target="tpu_custom_call" | custom-call | tf_op jit(solution)/shard_map/pallas_call | solution.py:227
  24.3 0.0 collective-permute-done.9.refs_1_.refs_7_
  24.3 0.1 shard_map.92.refs_11_
  24.5 2.0 %collective-permute-done.7.refs_5_ = bf16[2,64,512]{2,1,0:T(8,128)(2,1)S(1)} collective-permute-done((bf16[2,64,512]{2,1,0:T(8,128)(2,1)S(1)}, bf16[2,64,512]{2,1,0:T(8,128)(2,1)S(1)}, u32[]{:S(2)}, u32[]{:S(2)}) %collective-permute-start.7) | collective-permute-done | bytes 131104 | tf_op jit(solution)/shard_map/ppermute | solution.py:29
  26.5 0.5 %collective-permute-done.8.refs_6_ = bf16[2,64,512]{2,1,0:T(8,128)(2,1)S(1)} collective-permute-done((bf16[2,64,512]{2,1,0:T(8,128)(2,1)S(1)}, bf16[2,64,512]{2,1,0:T(8,128)(2,1)S(1)}, u32[]{:S(2)}, u32[]{:S(2)}) %collective-permute-start.8) | collective-permute-done | bytes 131104 | tf_op jit(solution)/shard_map/ppermute | solution.py:29
  27.0 0.0 collective-permute-done.10.refs_13_
  27.0 0.0 collective-permute-done.11.refs_15_
  27.0 0.0 copy-start
  27.0 0.0 copy-start.1
  27.0 1.4 %shard_map.93 = bf16[64,128]{1,0:T(8,128)(2,1)S(1)} custom-call(bf16[1,64,512]{2,1,0:T(8,128)(2,1)S(1)} %bitcast.15, bf16[1,64,512]{2,1,0:T(8,128)(2,1)S(1)} %bitcast.14, bf16[2,64,512]{2,1,0:T(8,128)(2,1)S(1)} %pad_maximum_fusion.1.refs_1_.refs_2_, bf16[3,64,512]{2,1,0:T(8,128)(2,1)S(1)} %pad_maximum_fusion.refs_2_.refs_3_, ...), custom_call_target="tpu_custom_call" | custom-call | tf_op jit(solution)/shard_map/pallas_call | solution.py:227
  28.4 2.8 %collective-permute-start.12 = (bf16[64,128]{1,0:T(8,128)(2,1)S(1)}, bf16[64,128]{1,0:T(8,128)(2,1)S(1)}, u32[]{:S(2)}, u32[]{:S(2)}) collective-permute-start(bf16[64,128]{1,0:T(8,128)(2,1)S(1)} %shard_map.93), channel_id=1, source_target_pairs={{0,16},{2,18},{4,20},{6,22},{8,24},{10,26},{12,28},{14,30},{16,0},... | collective-permute-start | bytes 49160 | tf_op jit(solution)/shard_map/ppermute | solution.py:29
  31.2 0.6 %collective-permute-start.13 = (bf16[64,128]{1,0:T(8,128)(2,1)S(1)}, bf16[64,128]{1,0:T(8,128)(2,1)S(1)}, u32[]{:S(2)}, u32[]{:S(2)}) collective-permute-start(bf16[64,128]{1,0:T(8,128)(2,1)S(1)} %shard_map.93), channel_id=1, source_target_pairs={{0,24},{2,26},{4,28},{6,30},{8,16},{10,18},{12,20},{14,22},{16,8},... | collective-permute-start | bytes 49160 | tf_op jit(solution)/shard_map/ppermute | solution.py:29
  31.9 0.1 collective-permute-start.14
  31.9 1.1 %collective-permute-done.12 = bf16[64,128]{1,0:T(8,128)(2,1)S(1)} collective-permute-done((bf16[64,128]{1,0:T(8,128)(2,1)S(1)}, bf16[64,128]{1,0:T(8,128)(2,1)S(1)}, u32[]{:S(2)}, u32[]{:S(2)}) %collective-permute-start.12) | collective-permute-done | bytes 16416 | tf_op jit(solution)/shard_map/ppermute | solution.py:29
  33.1 3.7 %collective-permute-done.13 = bf16[64,128]{1,0:T(8,128)(2,1)S(1)} collective-permute-done((bf16[64,128]{1,0:T(8,128)(2,1)S(1)}, bf16[64,128]{1,0:T(8,128)(2,1)S(1)}, u32[]{:S(2)}, u32[]{:S(2)}) %collective-permute-start.13) | collective-permute-done | bytes 16416 | tf_op jit(solution)/shard_map/ppermute | solution.py:29
  36.8 0.0 collective-permute-done.14
  36.8 1.6 %collective-permute-start.16 = (bf16[4,64,128]{2,1,0:T(8,128)(2,1)S(1)}, bf16[4,64,128]{2,1,0:T(8,128)(2,1)S(1)}, u32[]{:S(2)}, u32[]{:S(2)}) collective-permute-start(bf16[4,64,128]{2,1,0:T(8,128)(2,1)S(1)} %pad_maximum_fusion.2.own_ref), channel_id=1, source_target_pairs={{0,6},{2,4},{4,2},{6,0},{8,14},{10,12},{12,10},{14,8},{16,22},{18,... | collective-permute-start | bytes 196616 | tf_op jit(solution)/shard_map/ppermute | solution.py:29
  38.3 0.5 %collective-permute-start.17 = (bf16[4,64,128]{2,1,0:T(8,128)(2,1)S(1)}, bf16[4,64,128]{2,1,0:T(8,128)(2,1)S(1)}, u32[]{:S(2)}, u32[]{:S(2)}) collective-permute-start(bf16[4,64,128]{2,1,0:T(8,128)(2,1)S(1)} %pad_maximum_fusion.2.own_ref), channel_id=1, source_target_pairs={{0,4},{2,6},{4,0},{6,2},{8,12},{10,14},{12,8},{14,10},{16,20},{18,... | collective-permute-start | bytes 196616 | tf_op jit(solution)/shard_map/ppermute | solution.py:29
  38.9 1.5 %collective-permute-start.15 = (bf16[4,64,128]{2,1,0:T(8,128)(2,1)S(1)}, bf16[4,64,128]{2,1,0:T(8,128)(2,1)S(1)}, u32[]{:S(2)}, u32[]{:S(2)}) collective-permute-start(bf16[4,64,128]{2,1,0:T(8,128)(2,1)S(1)} %pad_maximum_fusion.2.own_ref), channel_id=1, source_target_pairs={{0,2},{2,0},{4,6},{6,4},{8,10},{10,8},{12,14},{14,12},{16,18},{18,... | collective-permute-start | bytes 196616 | tf_op jit(solution)/shard_map/ppermute | solution.py:29
  41.0 1.0 %collective-permute-done.16.refs_0_ = bf16[4,64,128]{2,1,0:T(8,128)(2,1)S(1)} collective-permute-done((bf16[4,64,128]{2,1,0:T(8,128)(2,1)S(1)}, bf16[4,64,128]{2,1,0:T(8,128)(2,1)S(1)}, u32[]{:S(2)}, u32[]{:S(2)}) %collective-permute-start.16) | collective-permute-done | bytes 65568 | tf_op jit(solution)/shard_map/ppermute | solution.py:29
  42.0 0.7 %collective-permute-done.17.refs_1_ = bf16[4,64,128]{2,1,0:T(8,128)(2,1)S(1)} collective-permute-done((bf16[4,64,128]{2,1,0:T(8,128)(2,1)S(1)}, bf16[4,64,128]{2,1,0:T(8,128)(2,1)S(1)}, u32[]{:S(2)}, u32[]{:S(2)}) %collective-permute-start.17) | collective-permute-done | bytes 65568 | tf_op jit(solution)/shard_map/ppermute | solution.py:29
  42.7 0.0 copy-done
  42.7 0.0 copy-done.1
  42.7 0.3 shard_map.94
  43.0 0.1 collective-permute-done.15.last_ref
  43.1 0.9 %shard_map.95 = bf16[64,512]{1,0:T(8,128)(2,1)} custom-call(bf16[4,64,128]{2,1,0:T(8,128)(2,1)S(1)} %pad_maximum_fusion.2.own_ref, bf16[4,64,128]{2,1,0:T(8,128)(2,1)S(1)} %collective-permute-done.15.last_ref, f32[64,512]{1,0:T(8,128)S(1)} %get-tuple-element.21.partial_ref, f32[8,512]{1,0:T(8,128)S(1)} %get-tuple-element.22.tanh_ref, ...), custom_call_target="tpu_custom_call" | custom-call | tf_op jit(solution)/shard_map/pallas_call | solution.py:227
  (3 shorter events, 0.0 us)
Async XLA Ops:
  0.0 8.9 %collective-permute-start.1 = (bf16[64,512]{1,0:T(8,128)(2,1)}, bf16[64,512]{1,0:T(8,128)(2,1)S(1)}, u32[]{:S(2)}, u32[]{:S(2)}) collective-permute-start(bf16[64,512]{1,0:T(8,128)(2,1)} %refs_3_.3), channel_id=1, source_target_pairs={{0,16},{2,18},{4,20},{6,22},{8,24},{10,26},{12,28},{14,30},{16,0},... | collective-permute-start | bytes 196616 | tf_op jit(solution)/shard_map/ppermute | solution.py:29
  4.1 6.4 %collective-permute-start.2 = (bf16[64,512]{1,0:T(8,128)(2,1)}, bf16[64,512]{1,0:T(8,128)(2,1)S(1)}, u32[]{:S(2)}, u32[]{:S(2)}) collective-permute-start(bf16[64,512]{1,0:T(8,128)(2,1)} %refs_3_.3), channel_id=1, source_target_pairs={{0,24},{2,26},{4,28},{6,30},{8,16},{10,18},{12,20},{14,22},{16,8},... | collective-permute-start | bytes 196616 | tf_op jit(solution)/shard_map/ppermute | solution.py:29
  5.4 5.5 %collective-permute-start.3 = (bf16[64,512]{1,0:T(8,128)(2,1)}, bf16[64,512]{1,0:T(8,128)(2,1)S(1)}, u32[]{:S(2)}, u32[]{:S(2)}) collective-permute-start(bf16[64,512]{1,0:T(8,128)(2,1)} %refs_3_.3), channel_id=1, source_target_pairs={{0,6},{2,4},{4,2},{6,0},{8,14},{10,12},{12,10},{14,8},{16,22},{18,... | collective-permute-start | bytes 196616 | tf_op jit(solution)/shard_map/ppermute | solution.py:29
  7.9 5.5 %collective-permute-start.4 = (bf16[64,512]{1,0:T(8,128)(2,1)}, bf16[64,512]{1,0:T(8,128)(2,1)S(1)}, u32[]{:S(2)}, u32[]{:S(2)}) collective-permute-start(bf16[64,512]{1,0:T(8,128)(2,1)} %refs_3_.3), channel_id=1, source_target_pairs={{0,4},{2,6},{4,0},{6,2},{8,12},{10,14},{12,8},{14,10},{16,20},{18,... | collective-permute-start | bytes 196616 | tf_op jit(solution)/shard_map/ppermute | solution.py:29
  8.4 5.0 %collective-permute-start.5 = (bf16[64,512]{1,0:T(8,128)(2,1)}, bf16[64,512]{1,0:T(8,128)(2,1)S(1)}, u32[]{:S(2)}, u32[]{:S(2)}) collective-permute-start(bf16[64,512]{1,0:T(8,128)(2,1)} %refs_3_.3), channel_id=1, source_target_pairs={{0,2},{2,0},{4,6},{6,4},{8,10},{10,8},{12,14},{14,12},{16,18},{18,... | collective-permute-start | bytes 196616 | tf_op jit(solution)/shard_map/ppermute | solution.py:29
  8.9 18.1 %collective-permute-start.10 = (bf16[16,64,128]{2,1,0:T(8,128)(2,1)}, bf16[16,64,128]{2,1,0:T(8,128)(2,1)S(1)}, u32[]{:S(2)}, u32[]{:S(2)}) collective-permute-start(bf16[16,64,128]{2,1,0:T(8,128)(2,1)} %refs_5_.1), channel_id=1, source_target_pairs={{0,1},{1,0},{2,3},{3,2},{4,5},{5,4},{6,7},{7,6},{8,9},{9,8},{10,11... | collective-permute-start | bytes 786440 | tf_op jit(solution)/shard_map/ppermute | solution.py:29
  10.4 16.6 %collective-permute-start.11 = (bf16[16,64,128]{2,1,0:T(8,128)(2,1)}, bf16[16,64,128]{2,1,0:T(8,128)(2,1)S(1)}, u32[]{:S(2)}, u32[]{:S(2)}) collective-permute-start(bf16[16,64,128]{2,1,0:T(8,128)(2,1)} %refs_6_.1), channel_id=1, source_target_pairs={{0,1},{1,0},{2,3},{3,2},{4,5},{5,4},{6,7},{7,6},{8,9},{9,8},{10,11... | collective-permute-start | bytes 786440 | tf_op jit(solution)/shard_map/ppermute | solution.py:29
  10.9 11.1 %collective-permute-start.6 = (bf16[2,64,512]{2,1,0:T(8,128)(2,1)S(1)}, bf16[2,64,512]{2,1,0:T(8,128)(2,1)S(1)}, u32[]{:S(2)}, u32[]{:S(2)}) collective-permute-start(bf16[2,64,512]{2,1,0:T(8,128)(2,1)S(1)} %pad_maximum_fusion.1.refs_1_.refs_2_), channel_id=1, source_target_pairs={{0,6},{2,4},{4,2},{6,0},{8,14},{10,12},{12,10},{14,8},{16,22},{18,... | collective-permute-start | bytes 393224 | tf_op jit(solution)/shard_map/ppermute | solution.py:29
  13.4 11.0 %collective-permute-start.9 = (bf16[3,64,512]{2,1,0:T(8,128)(2,1)S(1)}, bf16[3,64,512]{2,1,0:T(8,128)(2,1)S(1)}, u32[]{:S(2)}, u32[]{:S(2)}) collective-permute-start(bf16[3,64,512]{2,1,0:T(8,128)(2,1)S(1)} %pad_maximum_fusion.refs_2_.refs_3_), channel_id=1, source_target_pairs={{0,8},{2,10},{4,12},{6,14},{8,0},{10,2},{12,4},{14,6},{16,24},{18,... | collective-permute-start | bytes 589832 | tf_op jit(solution)/shard_map/ppermute | solution.py:29
  14.2 7.4 %collective-permute-start = (bf16[64,512]{1,0:T(8,128)(2,1)}, bf16[64,512]{1,0:T(8,128)(2,1)S(1)}, u32[]{:S(2)}, u32[]{:S(2)}) collective-permute-start(bf16[64,512]{1,0:T(8,128)(2,1)} %refs_3_.3), channel_id=1, source_target_pairs={{0,8},{2,10},{4,12},{6,14},{8,0},{10,2},{12,4},{14,6},{16,24},{18,... | collective-permute-start | bytes 196616 | tf_op jit(solution)/shard_map/ppermute | solution.py:29
  21.5 5.0 %collective-permute-start.7 = (bf16[2,64,512]{2,1,0:T(8,128)(2,1)S(1)}, bf16[2,64,512]{2,1,0:T(8,128)(2,1)S(1)}, u32[]{:S(2)}, u32[]{:S(2)}) collective-permute-start(bf16[2,64,512]{2,1,0:T(8,128)(2,1)S(1)} %pad_maximum_fusion.1.refs_1_.refs_2_), channel_id=1, source_target_pairs={{0,4},{2,6},{4,0},{6,2},{8,12},{10,14},{12,8},{14,10},{16,20},{18,... | collective-permute-start | bytes 393224 | tf_op jit(solution)/shard_map/ppermute | solution.py:29
  22.0 5.0 %collective-permute-start.8 = (bf16[2,64,512]{2,1,0:T(8,128)(2,1)S(1)}, bf16[2,64,512]{2,1,0:T(8,128)(2,1)S(1)}, u32[]{:S(2)}, u32[]{:S(2)}) collective-permute-start(bf16[2,64,512]{2,1,0:T(8,128)(2,1)S(1)} %pad_maximum_fusion.1.refs_1_.refs_2_), channel_id=1, source_target_pairs={{0,2},{2,0},{4,6},{6,4},{8,10},{10,8},{12,14},{14,12},{16,18},{18,... | collective-permute-start | bytes 393224 | tf_op jit(solution)/shard_map/ppermute | solution.py:29
  27.0 15.7 %copy-start = (bf16[2048,512]{1,0:T(8,128)(2,1)S(1)}, bf16[2048,512]{1,0:T(8,128)(2,1)}, u32[]{:S(2)}) copy-start(bf16[2048,512]{1,0:T(8,128)(2,1)} %weight_ref.1) | copy-start | bytes 6291460
  27.0 15.7 %copy-start.1 = (bf16[64,512]{1,0:T(8,128)(2,1)S(1)}, bf16[64,512]{1,0:T(8,128)(2,1)}, u32[]{:S(2)}) copy-start(bf16[64,512]{1,0:T(8,128)(2,1)} %refs_3_.3) | copy-start | bytes 196612
  28.4 4.7 %collective-permute-start.12 = (bf16[64,128]{1,0:T(8,128)(2,1)S(1)}, bf16[64,128]{1,0:T(8,128)(2,1)S(1)}, u32[]{:S(2)}, u32[]{:S(2)}) collective-permute-start(bf16[64,128]{1,0:T(8,128)(2,1)S(1)} %shard_map.93), channel_id=1, source_target_pairs={{0,16},{2,18},{4,20},{6,22},{8,24},{10,26},{12,28},{14,30},{16,0},... | collective-permute-start | bytes 49160 | tf_op jit(solution)/shard_map/ppermute | solution.py:29
  31.2 5.5 %collective-permute-start.13 = (bf16[64,128]{1,0:T(8,128)(2,1)S(1)}, bf16[64,128]{1,0:T(8,128)(2,1)S(1)}, u32[]{:S(2)}, u32[]{:S(2)}) collective-permute-start(bf16[64,128]{1,0:T(8,128)(2,1)S(1)} %shard_map.93), channel_id=1, source_target_pairs={{0,24},{2,26},{4,28},{6,30},{8,16},{10,18},{12,20},{14,22},{16,8},... | collective-permute-start | bytes 49160 | tf_op jit(solution)/shard_map/ppermute | solution.py:29
  31.9 4.9 %collective-permute-start.14 = (bf16[64,128]{1,0:T(8,128)(2,1)S(1)}, bf16[64,128]{1,0:T(8,128)(2,1)S(1)}, u32[]{:S(2)}, u32[]{:S(2)}) collective-permute-start(bf16[64,128]{1,0:T(8,128)(2,1)S(1)} %shard_map.93), channel_id=1, source_target_pairs={{0,8},{2,10},{4,12},{6,14},{8,0},{10,2},{12,4},{14,6},{16,24},{18,... | collective-permute-start | bytes 49160 | tf_op jit(solution)/shard_map/ppermute | solution.py:29
  36.8 5.2 %collective-permute-start.16 = (bf16[4,64,128]{2,1,0:T(8,128)(2,1)S(1)}, bf16[4,64,128]{2,1,0:T(8,128)(2,1)S(1)}, u32[]{:S(2)}, u32[]{:S(2)}) collective-permute-start(bf16[4,64,128]{2,1,0:T(8,128)(2,1)S(1)} %pad_maximum_fusion.2.own_ref), channel_id=1, source_target_pairs={{0,6},{2,4},{4,2},{6,0},{8,14},{10,12},{12,10},{14,8},{16,22},{18,... | collective-permute-start | bytes 196616 | tf_op jit(solution)/shard_map/ppermute | solution.py:29
  38.3 4.4 %collective-permute-start.17 = (bf16[4,64,128]{2,1,0:T(8,128)(2,1)S(1)}, bf16[4,64,128]{2,1,0:T(8,128)(2,1)S(1)}, u32[]{:S(2)}, u32[]{:S(2)}) collective-permute-start(bf16[4,64,128]{2,1,0:T(8,128)(2,1)S(1)} %pad_maximum_fusion.2.own_ref), channel_id=1, source_target_pairs={{0,4},{2,6},{4,0},{6,2},{8,12},{10,14},{12,8},{14,10},{16,20},{18,... | collective-permute-start | bytes 196616 | tf_op jit(solution)/shard_map/ppermute | solution.py:29
  38.9 4.3 %collective-permute-start.15 = (bf16[4,64,128]{2,1,0:T(8,128)(2,1)S(1)}, bf16[4,64,128]{2,1,0:T(8,128)(2,1)S(1)}, u32[]{:S(2)}, u32[]{:S(2)}) collective-permute-start(bf16[4,64,128]{2,1,0:T(8,128)(2,1)S(1)} %pad_maximum_fusion.2.own_ref), channel_id=1, source_target_pairs={{0,2},{2,0},{4,6},{6,4},{8,10},{10,8},{12,14},{14,12},{16,18},{18,... | collective-permute-start | bytes 196616 | tf_op jit(solution)/shard_map/ppermute | solution.py:29
